TPU v7x, 512 devices: a whole 4x8x8 slice. The times are simulated.
512 devices in a mesh: seq: 64 (over y_lo, x, z), head: 8 (over y_hi, core).
Axes of the slice: x: 4, y: 8 (y_hi: 4, y_lo: 2; y = y_hi * 2 + y_lo), z: 8, core: 2. Of those that a mesh axis runs over, the one named last changes fastest.
Arguments:
- queries: bfloat16 [16384, 3072], P(('seq', 'head')), may hold values from -6 to 6
- keys: bfloat16 [16384, 3072], P('seq', 'head'), may hold values from -6 to 6
- values: bfloat16 [16384, 3072], P('seq', 'head'), may hold values from -6 to 6
- window: int32 [64, 27], P('seq'), may hold values from -1 to 63, as said below
- out_weight: bfloat16 [3072, 6144], P('seq', 'head'), may hold values from -0.109375 to 0.109375
Outputs:
- projected: bfloat16 [16384, 6144], P('seq', 'head')
Inputs may be any that keep to these rules, and one draw needn't show every extreme that they name: Tile g lies at (g // 16, g // 4 % 4, g % 4) in a grid of 4 x 4 x 4 tiles. Entry k of window[g] is either -1 or the tile that lies (k // 9 - 1, k // 3 % 3 - 1, k % 3 - 1) steps away from g along time, height and width; it is -1 where that tile is outside the grid. Entry 13 is g itself.
All inputs are finite; a program needn't handle non-finite values.
Results may differ from a plain program's by a relative error of at most 0.0075.
Values may be sent and summed in bfloat16 or wider, within the bound.
A program may use at most 64 MiB of HBM per device.

v0:
```python
import jax
import jax.numpy as jnp
from jax import lax
from jax.sharding import PartitionSpec as P

HEAD_DIM = 128
GH = 4
GW = 4


def passed_along(array, axis, by):
    count = lax.axis_size(axis)
    pairs = [(i, i + by) for i in range(count) if 0 <= i + by < count]
    return lax.ppermute(array, axis, pairs)


def attend_block(softmax_state, queries, kv_block, live_keys):
    run_max, run_sum, run_acc = softmax_state
    factor = queries.shape[-1] ** (-0.5)
    scores = (
        jnp.einsum("qhd,khd->qhk", queries, kv_block[0], preferred_element_type=jnp.float32)
        * factor
    )
    scores = jnp.where(live_keys[None, None, :], scores, -1e30)
    new_max = jnp.maximum(run_max, jnp.max(scores, axis=-1))
    rescale = jnp.exp(run_max - new_max)
    weights = jnp.where(live_keys[None, None, :], jnp.exp(scores - new_max[:, :, None]), 0.0)
    run_sum = run_sum * rescale + jnp.sum(weights, axis=-1)
    run_acc = run_acc * rescale[:, :, None] + jnp.einsum(
        "qhk,khd->qhd",
        weights.astype(jnp.bfloat16),
        kv_block[1],
        preferred_element_type=jnp.float32,
    )
    return (new_max, run_sum, run_acc)


def local(queries, keys, values, window, out_weight):
    tok_rows = queries.shape[0]
    head_width = HEAD_DIM
    heads_all = queries.shape[1] // head_width
    local_q = lax.all_to_all(
        queries.reshape(tok_rows, heads_all, head_width),
        "head",
        split_axis=1,
        concat_axis=0,
        tiled=True,
    )
    tile_rows = local_q.shape[0]
    heads_dev = local_q.shape[1]
    live_tiles = window[0] >= 0
    kv_pair = jnp.stack(
        [
            keys.reshape(tile_rows, heads_dev, head_width),
            values.reshape(tile_rows, heads_dev, head_width),
        ]
    )
    softmax_state = (
        jnp.full((tile_rows, heads_dev), -1e30, jnp.float32),
        jnp.zeros((tile_rows, heads_dev), jnp.float32),
        jnp.zeros((tile_rows, heads_dev, head_width), jnp.float32),
    )
    seq_span = lax.axis_size("seq")
    plane_size = GH * GW

    def tile_mask(first_slot, tile_count):
        return jnp.repeat(live_tiles[first_slot : first_slot + tile_count], tile_rows)

    softmax_state = attend_block(softmax_state, local_q, kv_pair, tile_mask(13, 1))
    for slot_index in range(27):
        offset = (
            (slot_index // 9 - 1) * plane_size
            + (slot_index // 3 % 3 - 1) * GW
            + (slot_index % 3 - 1)
        )
        if slot_index != 13 and abs(offset) < seq_span:
            remote = passed_along(kv_pair, "seq", -offset)
            softmax_state = attend_block(softmax_state, local_q, remote, tile_mask(slot_index, 1))
    run_max, run_sum, run_acc = softmax_state
    finished = (run_acc / run_sum[:, :, None]).astype(jnp.bfloat16)
    finished = finished.reshape(tile_rows, heads_dev * head_width)
    all_heads = lax.all_gather(finished, "head", axis=1, tiled=True)
    projected = jnp.dot(
        all_heads,
        lax.all_gather(out_weight, "seq", axis=0, tiled=True),
        preferred_element_type=jnp.float32,
    )
    return projected.astype(jnp.bfloat16)


def solution(mesh):
    in_specs = (
        P(("seq", "head"), None),
        P("seq", "head"),
        P("seq", "head"),
        P("seq", None),
        P("seq", "head"),
    )
    out_specs = P("seq", "head")
    return jax.shard_map(local, mesh=mesh, in_specs=in_specs, out_specs=out_specs, check_vma=False)
```

profile of v0, /device:TPU:40, one launch (start us, length us, event | category | flops | bytes accessed | tf_op | source)
XLA Modules:
  0.0 854.6 jit_solution(16147548756407061988)
XLA Ops:
  9.1 9.6 %collective-permute-start.25 = (bf16[2,256,3,128]{3,1,2,0:T(8,128)(2,1)S(1)}, bf16[2,256,3,128]{3,1,2,0:T(8,128)(2,1)S(1)}, u32[]{:S(2)}, u32[]{:S(2)}) collective-permute-start(bf16[2,256,3,128]{3,1,2,0:T(8,128)(2,1)S(1)} %pad_maximum_fusion), channel_id=1, source_target_pairs={{168,0},{176,8},{184,16},{192,24},{200,32},{208,40},{216,48},{224,... | collective-permute-start | bytes 1179656 | tf_op jit(solution)/shard_map/ppermute | solution.py:14
  18.7 4.3 collective-permute-start.24
  23.0 1.9 collective-permute-start.23
  25.0 1.9 collective-permute-start.22
  26.9 1.9 collective-permute-start.21
  29.5 7.2 all-to-all-start
  38.8 74.6 %all-to-all-done = bf16[32,24,128]{2,0,1:T(8,128)(2,1)S(1)} async-done(((bf16[32,24,128]{2,0,1:T(8,128)(2,1)}), bf16[32,24,128]{2,0,1:T(8,128)(2,1)S(1)}, u32[]{:S(2)}, u32[]{:S(2)}) %all-to-all-start) | async-done | bytes 196640 | tf_op jit(solution)/shard_map/all_to_all | solution.py:42
  115.1 1.9 collective-permute-start.20
  118.0 1.9 collective-permute-start.19
  120.8 1.9 collective-permute-start.18
  123.7 1.9 collective-permute-start.17
  126.5 7.5 collective-permute-start.16
  135.0 34.0 %collective-permute-done.20 = bf16[2,256,3,128]{3,1,2,0:T(8,128)(2,1)S(1)} collective-permute-done((bf16[2,256,3,128]{3,1,2,0:T(8,128)(2,1)S(1)}, bf16[2,256,3,128]{3,1,2,0:T(8,128)(2,1)S(1)}, u32[]{:S(2)}, u32[]{:S(2)}) %collective-permute-start.20) | collective-permute-done | bytes 393248 | tf_op jit(solution)/shard_map/ppermute | solution.py:14
  169.0 1.9 collective-permute-start.15
  171.8 3.8 collective-permute-start.14
  176.5 25.9 %collective-permute-start.13 = (bf16[2,256,3,128]{3,1,2,0:T(8,128)(2,1)S(1)}, bf16[2,256,3,128]{3,1,2,0:T(8,128)(2,1)S(1)}, u32[]{:S(2)}, u32[]{:S(2)}) collective-permute-start(bf16[2,256,3,128]{3,1,2,0:T(8,128)(2,1)S(1)} %pad_maximum_fusion), channel_id=1, source_target_pairs={{8,0},{16,8},{24,16},{32,24},{40,32},{48,40},{56,48},{64,56},{72,6... | collective-permute-start | bytes 1179656 | tf_op jit(solution)/shard_map/ppermute | solution.py:14
  203.3 1.9 collective-permute-start.12
  206.1 11.2 %collective-permute-done.16 = bf16[2,256,3,128]{3,1,2,0:T(8,128)(2,1)S(1)} collective-permute-done((bf16[2,256,3,128]{3,1,2,0:T(8,128)(2,1)S(1)}, bf16[2,256,3,128]{3,1,2,0:T(8,128)(2,1)S(1)}, u32[]{:S(2)}, u32[]{:S(2)}) %collective-permute-start.16) | collective-permute-done | bytes 393248 | tf_op jit(solution)/shard_map/ppermute | solution.py:14
  217.3 3.9 collective-permute-start.11
  222.1 12.0 %collective-permute-done.15 = bf16[2,256,3,128]{3,1,2,0:T(8,128)(2,1)S(1)} collective-permute-done((bf16[2,256,3,128]{3,1,2,0:T(8,128)(2,1)S(1)}, bf16[2,256,3,128]{3,1,2,0:T(8,128)(2,1)S(1)}, u32[]{:S(2)}, u32[]{:S(2)}) %collective-permute-start.15) | collective-permute-done | bytes 393248 | tf_op jit(solution)/shard_map/ppermute | solution.py:14
  234.1 1.9 collective-permute-start.10
  237.0 21.6 %collective-permute-done.14 = bf16[2,256,3,128]{3,1,2,0:T(8,128)(2,1)S(1)} collective-permute-done((bf16[2,256,3,128]{3,1,2,0:T(8,128)(2,1)S(1)}, bf16[2,256,3,128]{3,1,2,0:T(8,128)(2,1)S(1)}, u32[]{:S(2)}, u32[]{:S(2)}) %collective-permute-start.14) | collective-permute-done | bytes 393248 | tf_op jit(solution)/shard_map/ppermute | solution.py:14
  258.5 1.9 collective-permute-start.9
  261.4 9.2 %collective-permute-done.13 = bf16[2,256,3,128]{3,1,2,0:T(8,128)(2,1)S(1)} collective-permute-done((bf16[2,256,3,128]{3,1,2,0:T(8,128)(2,1)S(1)}, bf16[2,256,3,128]{3,1,2,0:T(8,128)(2,1)S(1)}, u32[]{:S(2)}, u32[]{:S(2)}) %collective-permute-start.13) | collective-permute-done | bytes 393248 | tf_op jit(solution)/shard_map/ppermute | solution.py:14
  270.7 1.9 collective-permute-start.8
  273.4 13.6 %collective-permute-start.7 = (bf16[2,256,3,128]{3,1,2,0:T(8,128)(2,1)S(1)}, bf16[2,256,3,128]{3,1,2,0:T(8,128)(2,1)S(1)}, u32[]{:S(2)}, u32[]{:S(2)}) collective-permute-start(bf16[2,256,3,128]{3,1,2,0:T(8,128)(2,1)S(1)} %pad_maximum_fusion), channel_id=1, source_target_pairs={{0,96},{8,104},{16,112},{24,120},{32,128},{40,136},{48,144},{56,15... | collective-permute-start | bytes 1179656 | tf_op jit(solution)/shard_map/ppermute | solution.py:14
  287.9 8.7 %collective-permute-start.6 = (bf16[2,256,3,128]{3,1,2,0:T(8,128)(2,1)S(1)}, bf16[2,256,3,128]{3,1,2,0:T(8,128)(2,1)S(1)}, u32[]{:S(2)}, u32[]{:S(2)}) collective-permute-start(bf16[2,256,3,128]{3,1,2,0:T(8,128)(2,1)S(1)} %pad_maximum_fusion), channel_id=1, source_target_pairs={{0,104},{8,112},{16,120},{24,128},{32,136},{40,144},{48,152},{56,1... | collective-permute-start | bytes 1179656 | tf_op jit(solution)/shard_map/ppermute | solution.py:14
  297.5 47.2 %collective-permute-start.5 = (bf16[2,256,3,128]{3,1,2,0:T(8,128)(2,1)S(1)}, bf16[2,256,3,128]{3,1,2,0:T(8,128)(2,1)S(1)}, u32[]{:S(2)}, u32[]{:S(2)}) collective-permute-start(bf16[2,256,3,128]{3,1,2,0:T(8,128)(2,1)S(1)} %pad_maximum_fusion), channel_id=1, source_target_pairs={{0,120},{8,128},{16,136},{24,144},{32,152},{40,160},{48,168},{56,1... | collective-permute-start | bytes 1179656 | tf_op jit(solution)/shard_map/ppermute | solution.py:14
  345.7 1.9 collective-permute-start.4
  348.5 1.9 collective-permute-start.3
  351.4 1.9 collective-permute-start.2
  354.2 3.7 collective-permute-start.1
  358.9 32.7 %collective-permute-done.5 = bf16[2,256,3,128]{3,1,2,0:T(8,128)(2,1)S(1)} collective-permute-done((bf16[2,256,3,128]{3,1,2,0:T(8,128)(2,1)S(1)}, bf16[2,256,3,128]{3,1,2,0:T(8,128)(2,1)S(1)}, u32[]{:S(2)}, u32[]{:S(2)}) %collective-permute-start.5) | collective-permute-done | bytes 393248 | tf_op jit(solution)/shard_map/ppermute | solution.py:14
  391.5 2.1 collective-permute-start
  398.2 7.1 collective-permute-done
  406.4 1.6 fusion.159
  408.0 1.5 fusion.155
  409.5 1.5 fusion.151
  411.0 1.5 fusion.147
  414.0 1.7 fusion.139
  417.1 1.5 fusion.131
  418.6 1.6 fusion.127
  421.7 1.5 fusion.119
  424.6 1.7 fusion.111
  449.8 2.5 fusion.108
  453.1 77.9 %all-gather.3.cloned.1.call-done = bf16[256,3072]{0,1:T(8,128)(2,1)} async-done(((bf16[256,384]{0,1:T(8,128)(2,1)}), bf16[256,3072]{0,1:T(8,128)(2,1)}) %all-gather.3.cloned.1.call-update) | async-done | bytes 1572880 | tf_op jit(solution)/shard_map/all_gather | solution.py:82
  531.0 311.7 %all-gather.5.cloned.1.call-done = bf16[3072,768]{1,0:T(8,128)(2,1)} async-done(((bf16[48,768]{1,0:T(8,128)(2,1)}), bf16[3072,768]{1,0:T(8,128)(2,1)}) %all-gather.5.cloned.1.call-update) | async-done | bytes 4718608 | tf_op jit(solution)/shard_map/all_gather | solution.py:85
  842.8 5.0 convolution_convert_fusion
  (96 shorter events, 60.6 us)
Async XLA Ops:
  6.5 22.3 %copy-start = (bf16[32,3072]{1,0:T(8,128)(2,1)S(1)}, bf16[32,3072]{1,0:T(8,128)(2,1)}, u32[]{:S(2)}) copy-start(bf16[32,3072]{1,0:T(8,128)(2,1)} %param.5) | copy-start | bytes 589828
  9.1 106.0 %collective-permute-start.25 = (bf16[2,256,3,128]{3,1,2,0:T(8,128)(2,1)S(1)}, bf16[2,256,3,128]{3,1,2,0:T(8,128)(2,1)S(1)}, u32[]{:S(2)}, u32[]{:S(2)}) collective-permute-start(bf16[2,256,3,128]{3,1,2,0:T(8,128)(2,1)S(1)} %pad_maximum_fusion), channel_id=1, source_target_pairs={{168,0},{176,8},{184,16},{192,24},{200,32},{208,40},{216,48},{224,... | collective-permute-start | bytes 1179656 | tf_op jit(solution)/shard_map/ppermute | solution.py:14
  18.7 99.3 %collective-permute-start.24 = (bf16[2,256,3,128]{3,1,2,0:T(8,128)(2,1)S(1)}, bf16[2,256,3,128]{3,1,2,0:T(8,128)(2,1)S(1)}, u32[]{:S(2)}, u32[]{:S(2)}) collective-permute-start(bf16[2,256,3,128]{3,1,2,0:T(8,128)(2,1)S(1)} %pad_maximum_fusion), channel_id=1, source_target_pairs={{160,0},{168,8},{176,16},{184,24},{192,32},{200,40},{208,48},{216,... | collective-permute-start | bytes 1179656 | tf_op jit(solution)/shard_map/ppermute | solution.py:14
  23.0 97.8 %collective-permute-start.23 = (bf16[2,256,3,128]{3,1,2,0:T(8,128)(2,1)S(1)}, bf16[2,256,3,128]{3,1,2,0:T(8,128)(2,1)S(1)}, u32[]{:S(2)}, u32[]{:S(2)}) collective-permute-start(bf16[2,256,3,128]{3,1,2,0:T(8,128)(2,1)S(1)} %pad_maximum_fusion), channel_id=1, source_target_pairs={{152,0},{160,8},{168,16},{176,24},{184,32},{192,40},{200,48},{208,... | collective-permute-start | bytes 1179656 | tf_op jit(solution)/shard_map/ppermute | solution.py:14
  25.0 98.7 %collective-permute-start.22 = (bf16[2,256,3,128]{3,1,2,0:T(8,128)(2,1)S(1)}, bf16[2,256,3,128]{3,1,2,0:T(8,128)(2,1)S(1)}, u32[]{:S(2)}, u32[]{:S(2)}) collective-permute-start(bf16[2,256,3,128]{3,1,2,0:T(8,128)(2,1)S(1)} %pad_maximum_fusion), channel_id=1, source_target_pairs={{136,0},{144,8},{152,16},{160,24},{168,32},{176,40},{184,48},{192,... | collective-permute-start | bytes 1179656 | tf_op jit(solution)/shard_map/ppermute | solution.py:14
  26.9 99.7 %collective-permute-start.21 = (bf16[2,256,3,128]{3,1,2,0:T(8,128)(2,1)S(1)}, bf16[2,256,3,128]{3,1,2,0:T(8,128)(2,1)S(1)}, u32[]{:S(2)}, u32[]{:S(2)}) collective-permute-start(bf16[2,256,3,128]{3,1,2,0:T(8,128)(2,1)S(1)} %pad_maximum_fusion), channel_id=1, source_target_pairs={{128,0},{136,8},{144,16},{152,24},{160,32},{168,40},{176,48},{184,... | collective-permute-start | bytes 1179656 | tf_op jit(solution)/shard_map/ppermute | solution.py:14
  29.5 83.9 %all-to-all-start = ((bf16[32,24,128]{2,0,1:T(8,128)(2,1)}), bf16[32,24,128]{2,0,1:T(8,128)(2,1)S(1)}, u32[]{:S(2)}, u32[]{:S(2)}) async-start(bf16[32,24,128]{2,0,1:T(8,128)(2,1)} %copy_bitcast_fusion), calls=%async_computation | async-start | bytes 393216 | tf_op jit(solution)/shard_map/all_to_all | solution.py:42
  36.7 494.3 %all-gather.3.cloned.1.call-start = ((), (), s32[]{:S(2)}) async-start(), calls=%async_computation.1 | async-start | bytes 1769472 | tf_op jit(solution)/shard_map/all_gather | solution.py:82
  115.1 53.9 %collective-permute-start.20 = (bf16[2,256,3,128]{3,1,2,0:T(8,128)(2,1)S(1)}, bf16[2,256,3,128]{3,1,2,0:T(8,128)(2,1)S(1)}, u32[]{:S(2)}, u32[]{:S(2)}) collective-permute-start(bf16[2,256,3,128]{3,1,2,0:T(8,128)(2,1)S(1)} %pad_maximum_fusion), channel_id=1, source_target_pairs={{120,0},{128,8},{136,16},{144,24},{152,32},{160,40},{168,48},{176,... | collective-permute-start | bytes 1179656 | tf_op jit(solution)/shard_map/ppermute | solution.py:14
  118.0 53.8 %collective-permute-start.19 = (bf16[2,256,3,128]{3,1,2,0:T(8,128)(2,1)S(1)}, bf16[2,256,3,128]{3,1,2,0:T(8,128)(2,1)S(1)}, u32[]{:S(2)}, u32[]{:S(2)}) collective-permute-start(bf16[2,256,3,128]{3,1,2,0:T(8,128)(2,1)S(1)} %pad_maximum_fusion), channel_id=1, source_target_pairs={{104,0},{112,8},{120,16},{128,24},{136,32},{144,40},{152,48},{160,... | collective-permute-start | bytes 1179656 | tf_op jit(solution)/shard_map/ppermute | solution.py:14
  120.8 55.7 %collective-permute-start.18 = (bf16[2,256,3,128]{3,1,2,0:T(8,128)(2,1)S(1)}, bf16[2,256,3,128]{3,1,2,0:T(8,128)(2,1)S(1)}, u32[]{:S(2)}, u32[]{:S(2)}) collective-permute-start(bf16[2,256,3,128]{3,1,2,0:T(8,128)(2,1)S(1)} %pad_maximum_fusion), channel_id=1, source_target_pairs={{96,0},{104,8},{112,16},{120,24},{128,32},{136,40},{144,48},{152,5... | collective-permute-start | bytes 1179656 | tf_op jit(solution)/shard_map/ppermute | solution.py:14
  123.7 79.6 %collective-permute-start.17 = (bf16[2,256,3,128]{3,1,2,0:T(8,128)(2,1)S(1)}, bf16[2,256,3,128]{3,1,2,0:T(8,128)(2,1)S(1)}, u32[]{:S(2)}, u32[]{:S(2)}) collective-permute-start(bf16[2,256,3,128]{3,1,2,0:T(8,128)(2,1)S(1)} %pad_maximum_fusion), channel_id=1, source_target_pairs={{88,0},{96,8},{104,16},{112,24},{120,32},{128,40},{136,48},{144,56... | collective-permute-start | bytes 1179656 | tf_op jit(solution)/shard_map/ppermute | solution.py:14
  126.5 90.8 %collective-permute-start.16 = (bf16[2,256,3,128]{3,1,2,0:T(8,128)(2,1)S(1)}, bf16[2,256,3,128]{3,1,2,0:T(8,128)(2,1)S(1)}, u32[]{:S(2)}, u32[]{:S(2)}) collective-permute-start(bf16[2,256,3,128]{3,1,2,0:T(8,128)(2,1)S(1)} %pad_maximum_fusion), channel_id=1, source_target_pairs={{40,0},{48,8},{56,16},{64,24},{72,32},{80,40},{88,48},{96,56},{104... | collective-permute-start | bytes 1179656 | tf_op jit(solution)/shard_map/ppermute | solution.py:14
  169.0 65.1 %collective-permute-start.15 = (bf16[2,256,3,128]{3,1,2,0:T(8,128)(2,1)S(1)}, bf16[2,256,3,128]{3,1,2,0:T(8,128)(2,1)S(1)}, u32[]{:S(2)}, u32[]{:S(2)}) collective-permute-start(bf16[2,256,3,128]{3,1,2,0:T(8,128)(2,1)S(1)} %pad_maximum_fusion), channel_id=1, source_target_pairs={{32,0},{40,8},{48,16},{56,24},{64,32},{72,40},{80,48},{88,56},{96,... | collective-permute-start | bytes 1179656 | tf_op jit(solution)/shard_map/ppermute | solution.py:14
  171.8 86.8 %collective-permute-start.14 = (bf16[2,256,3,128]{3,1,2,0:T(8,128)(2,1)S(1)}, bf16[2,256,3,128]{3,1,2,0:T(8,128)(2,1)S(1)}, u32[]{:S(2)}, u32[]{:S(2)}) collective-permute-start(bf16[2,256,3,128]{3,1,2,0:T(8,128)(2,1)S(1)} %pad_maximum_fusion), channel_id=1, source_target_pairs={{24,0},{32,8},{40,16},{48,24},{56,32},{64,40},{72,48},{80,56},{88,... | collective-permute-start | bytes 1179656 | tf_op jit(solution)/shard_map/ppermute | solution.py:14
  176.5 94.2 %collective-permute-start.13 = (bf16[2,256,3,128]{3,1,2,0:T(8,128)(2,1)S(1)}, bf16[2,256,3,128]{3,1,2,0:T(8,128)(2,1)S(1)}, u32[]{:S(2)}, u32[]{:S(2)}) collective-permute-start(bf16[2,256,3,128]{3,1,2,0:T(8,128)(2,1)S(1)} %pad_maximum_fusion), channel_id=1, source_target_pairs={{8,0},{16,8},{24,16},{32,24},{40,32},{48,40},{56,48},{64,56},{72,6... | collective-permute-start | bytes 1179656 | tf_op jit(solution)/shard_map/ppermute | solution.py:14
  203.3 70.1 %collective-permute-start.12 = (bf16[2,256,3,128]{3,1,2,0:T(8,128)(2,1)S(1)}, bf16[2,256,3,128]{3,1,2,0:T(8,128)(2,1)S(1)}, u32[]{:S(2)}, u32[]{:S(2)}) collective-permute-start(bf16[2,256,3,128]{3,1,2,0:T(8,128)(2,1)S(1)} %pad_maximum_fusion), channel_id=1, source_target_pairs={{0,8},{8,16},{16,24},{24,32},{32,40},{40,48},{48,56},{56,64},{64,7... | collective-permute-start | bytes 1179656 | tf_op jit(solution)/shard_map/ppermute | solution.py:14
  217.3 70.5 %collective-permute-start.11 = (bf16[2,256,3,128]{3,1,2,0:T(8,128)(2,1)S(1)}, bf16[2,256,3,128]{3,1,2,0:T(8,128)(2,1)S(1)}, u32[]{:S(2)}, u32[]{:S(2)}) collective-permute-start(bf16[2,256,3,128]{3,1,2,0:T(8,128)(2,1)S(1)} %pad_maximum_fusion), channel_id=1, source_target_pairs={{0,24},{8,32},{16,40},{24,48},{32,56},{40,64},{48,72},{56,80},{64,... | collective-permute-start | bytes 1179656 | tf_op jit(solution)/shard_map/ppermute | solution.py:14
  234.1 63.4 %collective-permute-start.10 = (bf16[2,256,3,128]{3,1,2,0:T(8,128)(2,1)S(1)}, bf16[2,256,3,128]{3,1,2,0:T(8,128)(2,1)S(1)}, u32[]{:S(2)}, u32[]{:S(2)}) collective-permute-start(bf16[2,256,3,128]{3,1,2,0:T(8,128)(2,1)S(1)} %pad_maximum_fusion), channel_id=1, source_target_pairs={{0,32},{8,40},{16,48},{24,56},{32,64},{40,72},{48,80},{56,88},{64,... | collective-permute-start | bytes 1179656 | tf_op jit(solution)/shard_map/ppermute | solution.py:14
  258.5 87.1 %collective-permute-start.9 = (bf16[2,256,3,128]{3,1,2,0:T(8,128)(2,1)S(1)}, bf16[2,256,3,128]{3,1,2,0:T(8,128)(2,1)S(1)}, u32[]{:S(2)}, u32[]{:S(2)}) collective-permute-start(bf16[2,256,3,128]{3,1,2,0:T(8,128)(2,1)S(1)} %pad_maximum_fusion), channel_id=1, source_target_pairs={{0,40},{8,48},{16,56},{24,64},{32,72},{40,80},{48,88},{56,96},{64,... | collective-permute-start | bytes 1179656 | tf_op jit(solution)/shard_map/ppermute | solution.py:14
  270.7 77.9 %collective-permute-start.8 = (bf16[2,256,3,128]{3,1,2,0:T(8,128)(2,1)S(1)}, bf16[2,256,3,128]{3,1,2,0:T(8,128)(2,1)S(1)}, u32[]{:S(2)}, u32[]{:S(2)}) collective-permute-start(bf16[2,256,3,128]{3,1,2,0:T(8,128)(2,1)S(1)} %pad_maximum_fusion), channel_id=1, source_target_pairs={{0,88},{8,96},{16,104},{24,112},{32,120},{40,128},{48,136},{56,144... | collective-permute-start | bytes 1179656 | tf_op jit(solution)/shard_map/ppermute | solution.py:14
  273.4 78.0 %collective-permute-start.7 = (bf16[2,256,3,128]{3,1,2,0:T(8,128)(2,1)S(1)}, bf16[2,256,3,128]{3,1,2,0:T(8,128)(2,1)S(1)}, u32[]{:S(2)}, u32[]{:S(2)}) collective-permute-start(bf16[2,256,3,128]{3,1,2,0:T(8,128)(2,1)S(1)} %pad_maximum_fusion), channel_id=1, source_target_pairs={{0,96},{8,104},{16,112},{24,120},{32,128},{40,136},{48,144},{56,15... | collective-permute-start | bytes 1179656 | tf_op jit(solution)/shard_map/ppermute | solution.py:14
  287.9 66.3 %collective-permute-start.6 = (bf16[2,256,3,128]{3,1,2,0:T(8,128)(2,1)S(1)}, bf16[2,256,3,128]{3,1,2,0:T(8,128)(2,1)S(1)}, u32[]{:S(2)}, u32[]{:S(2)}) collective-permute-start(bf16[2,256,3,128]{3,1,2,0:T(8,128)(2,1)S(1)} %pad_maximum_fusion), channel_id=1, source_target_pairs={{0,104},{8,112},{16,120},{24,128},{32,136},{40,144},{48,152},{56,1... | collective-permute-start | bytes 1179656 | tf_op jit(solution)/shard_map/ppermute | solution.py:14
  297.5 94.0 %collective-permute-start.5 = (bf16[2,256,3,128]{3,1,2,0:T(8,128)(2,1)S(1)}, bf16[2,256,3,128]{3,1,2,0:T(8,128)(2,1)S(1)}, u32[]{:S(2)}, u32[]{:S(2)}) collective-permute-start(bf16[2,256,3,128]{3,1,2,0:T(8,128)(2,1)S(1)} %pad_maximum_fusion), channel_id=1, source_target_pairs={{0,120},{8,128},{16,136},{24,144},{32,152},{40,160},{48,168},{56,1... | collective-permute-start | bytes 1179656 | tf_op jit(solution)/shard_map/ppermute | solution.py:14
  345.7 48.9 %collective-permute-start.4 = (bf16[2,256,3,128]{3,1,2,0:T(8,128)(2,1)S(1)}, bf16[2,256,3,128]{3,1,2,0:T(8,128)(2,1)S(1)}, u32[]{:S(2)}, u32[]{:S(2)}) collective-permute-start(bf16[2,256,3,128]{3,1,2,0:T(8,128)(2,1)S(1)} %pad_maximum_fusion), channel_id=1, source_target_pairs={{0,128},{8,136},{16,144},{24,152},{32,160},{40,168},{48,176},{56,1... | collective-permute-start | bytes 1179656 | tf_op jit(solution)/shard_map/ppermute | solution.py:14
  348.5 46.9 %collective-permute-start.3 = (bf16[2,256,3,128]{3,1,2,0:T(8,128)(2,1)S(1)}, bf16[2,256,3,128]{3,1,2,0:T(8,128)(2,1)S(1)}, u32[]{:S(2)}, u32[]{:S(2)}) collective-permute-start(bf16[2,256,3,128]{3,1,2,0:T(8,128)(2,1)S(1)} %pad_maximum_fusion), channel_id=1, source_target_pairs={{0,136},{8,144},{16,152},{24,160},{32,168},{40,176},{48,184},{56,1... | collective-permute-start | bytes 1179656 | tf_op jit(solution)/shard_map/ppermute | solution.py:14
  351.4 44.9 %collective-permute-start.2 = (bf16[2,256,3,128]{3,1,2,0:T(8,128)(2,1)S(1)}, bf16[2,256,3,128]{3,1,2,0:T(8,128)(2,1)S(1)}, u32[]{:S(2)}, u32[]{:S(2)}) collective-permute-start(bf16[2,256,3,128]{3,1,2,0:T(8,128)(2,1)S(1)} %pad_maximum_fusion), channel_id=1, source_target_pairs={{0,152},{8,160},{16,168},{24,176},{32,184},{40,192},{48,200},{56,2... | collective-permute-start | bytes 1179656 | tf_op jit(solution)/shard_map/ppermute | solution.py:14
  354.2 43.0 %collective-permute-start.1 = (bf16[2,256,3,128]{3,1,2,0:T(8,128)(2,1)S(1)}, bf16[2,256,3,128]{3,1,2,0:T(8,128)(2,1)S(1)}, u32[]{:S(2)}, u32[]{:S(2)}) collective-permute-start(bf16[2,256,3,128]{3,1,2,0:T(8,128)(2,1)S(1)} %pad_maximum_fusion), channel_id=1, source_target_pairs={{0,160},{8,168},{16,176},{24,184},{32,192},{40,200},{48,208},{56,2... | collective-permute-start | bytes 1179656 | tf_op jit(solution)/shard_map/ppermute | solution.py:14
  391.5 13.8 %collective-permute-start = (bf16[2,256,3,128]{3,1,2,0:T(8,128)(2,1)S(1)}, bf16[2,256,3,128]{3,1,2,0:T(8,128)(2,1)S(1)}, u32[]{:S(2)}, u32[]{:S(2)}) collective-permute-start(bf16[2,256,3,128]{3,1,2,0:T(8,128)(2,1)S(1)} %pad_maximum_fusion), channel_id=1, source_target_pairs={{0,168},{8,176},{16,184},{24,192},{32,200},{40,208},{48,216},{56,2... | collective-permute-start | bytes 1179656 | tf_op jit(solution)/shard_map/ppermute | solution.py:14
  452.3 390.4 %all-gather.5.cloned.1.call-start = ((), (), s32[]{:S(2)}) async-start(), calls=%async_computation.2 | async-start | bytes 4792320 | tf_op jit(solution)/shard_map/all_gather | solution.py:85
Sparse Core Ops, SparseCore 0:
  452.4 78.5 all-gather.2
  533.1 309.6 all-gather.4
where the time goes:
time: 857 us; the launch traced here: 855 us
  waiting for transfers between devices  593 us (69%)
  starting transfers between devices  166 us (19%)
  matrix products  55.1 us (6%)
  other arithmetic  21.5 us (3%)
  between operations  14.1 us (2%)
    all_gather x1, waiting for transfers between devices, local(): lax.all_gather(out_weight, 'seq', axis=0, tiled=True)  312 us
    ppermute x26, starting transfers between devices, passed_along(): return lax.ppermute(array, axis, pairs)  159 us
    ppermute x26, waiting for transfers between devices, passed_along(): return lax.ppermute(array, axis, pairs)  128 us
    all_gather x1, waiting for transfers between devices, local(): all_heads = lax.all_gather(finished, 'head', axis=1, tiled=True)  77.9 us
    all_to_all x1, waiting for transfers between devices, local(): lax.all_to_all(queries.reshape(tok_rows, heads_all, head_width), 'head',...  74.6 us
    dot_general x27, matrix products, attend_block(): jnp.einsum('qhk,khd->qhd', weights.astype(jnp.bfloat16), kv_block[1], pre...  25.7 us
    dot_general x27, matrix products, attend_block(): jnp.einsum('qhd,khd->qhk', queries, kv_block[0], preferred_element_type=j...  24.4 us
    reduce_sum x14, other arithmetic, attend_block(): run_sum = run_sum * rescale + jnp.sum(weights, axis=-1)  20.6 us
  transfers between devices with their start and end apart: 29, of which 10 were waited for; matrix products, arithmetic and copies ran while one was open for 3% of the time, Pallas kernels for 0%

commit v1 on v0

v1 whole, which is shorter than its diff:
```python
import functools

import jax
import jax.numpy as jnp
from jax import lax
from jax.experimental import pallas as pl
from jax.experimental.pallas import tpu as pltpu
from jax.sharding import PartitionSpec as P

MESH = pl.DeviceIdType.MESH
TILE = 256
HD = 128
HEADS_DEV = 3
WIDTH = HD * HEADS_DEV
GROUPS = 8
NEG = -1e30
BIG = 1e30
SCALE = 1.4426950408889634 * HD**-0.5
N_CH = 160


def kernel(q_in, k_in, v_in, bias_in, w_in, out_ref,
           kb, vb, wb, qb, bb, ab, sb, po, ps, ro, rs, lo, ls, send_sem, recv_sem, loc_sem):
    s = lax.axis_index("seq")
    g = lax.axis_index("head")
    y = s // 32
    x = (s // 8) % 4
    z = s % 8
    t = 2 * y + x // 2
    h = 2 * (x % 2) + z // 4
    w = z % 4
    core = g % 2

    def at(yy, xx, zz):
        return (yy * 32 + xx * 8 + zz, g)

    def at_time(tt):
        return (16 * tt + s % 16, g)

    z_up, z_dn = at(y, x, (z + 1) % 8), at(y, x, (z + 7) % 8)
    x_up, x_dn = at(y, (x + 1) % 4, z), at(y, (x + 3) % 4, z)
    x_flip = at(y, x + 1 - 2 * (x % 2), z)
    y_flip = at(1 - y, x, z)
    t_up, t_dn = at_time((t + 1) % 4), at_time((t + 3) % 4)
    partner = (s, g + 1 - 2 * core)

    def peer(d):
        return (s, (g + d) % GROUPS)

    barrier = pltpu.get_barrier_semaphore()
    greeted = [z_up, z_dn, x_up, x_dn, y_flip, t_up, t_dn] + [peer(d) for d in range(1, GROUPS)]
    for other in greeted:
        pl.semaphore_signal(barrier, inc=1, device_id=other, device_id_type=MESH)

    channels = [0]
    sent = []

    def channel(n=1):
        channels[0] += n
        return channels[0] - n

    def copy(src, dst, ch, dev):
        return pltpu.make_async_remote_copy(
            src_ref=src, dst_ref=dst, send_sem=send_sem.at[ch], recv_sem=recv_sem.at[ch],
            device_id=dev, device_id_type=MESH)

    def send(src, dst, ch, dev, cond=None):
        c = copy(src, dst, ch, dev)
        if cond is None:
            c.start()
        else:
            pl.when(cond)(c.start)
        sent.append((c, cond))

    def arrive(dst, ch, cond=None):
        c = copy(dst, dst, ch, z_up)
        if cond is None:
            c.wait_recv()
        else:
            pl.when(cond)(c.wait_recv)

    base = 8 * (x % 2)
    own = base + z
    row0 = pl.multiple_of(g * 32, 32)
    col0 = pl.multiple_of(g * WIDTH, HD)
    local = [
        pltpu.make_async_copy(k_in, kb.at[own], loc_sem.at[0]),
        pltpu.make_async_copy(v_in, vb.at[own], loc_sem.at[1]),
        pltpu.make_async_copy(w_in, wb.at[x, y, z], loc_sem.at[2]),
        pltpu.make_async_copy(q_in.at[:, pl.ds(col0, WIDTH)], qb.at[0, pl.ds(row0, 32)], loc_sem.at[3]),
        pltpu.make_async_copy(bias_in, bb.at[0], loc_sem.at[4]),
    ]
    for c in local:
        c.start()
    pl.semaphore_wait(barrier, len(greeted))

    q_ch = channel(GROUPS)
    for d in range(1, GROUPS):
        col = pl.multiple_of(((g + d) % GROUPS) * WIDTH, HD)
        send(q_in.at[:, pl.ds(col, WIDTH)], qb.at[0, pl.ds(row0, 32)], q_ch + d, peer(d))
    up_k, up_v, dn_k, dn_v = channel(5), channel(5), channel(5), channel(5)
    send(k_in, kb.at[own], up_k + 1, z_up)
    send(k_in, kb.at[own], dn_k + 1, z_dn)
    send(v_in, vb.at[own], up_v + 1, z_up)
    send(v_in, vb.at[own], dn_v + 1, z_dn)
    w_y = channel()
    send(w_in, wb.at[x, y, z], w_y, y_flip)
    for c in local:
        c.wait()

    later, earlier = t < 3, t > 0
    for d in range(1, GROUPS):
        src_row = pl.multiple_of(((g + GROUPS - d) % GROUPS) * 32, 32)
        arrive(qb.at[0, pl.ds(src_row, 32)], q_ch + d)
    q_up, q_dn, b_up, b_dn = channel(), channel(), channel(), channel()
    send(qb.at[0], qb.at[1], q_up, t_up, later)
    send(bb.at[0], bb.at[1], b_up, t_up, later)
    send(qb.at[0], qb.at[2], q_dn, t_dn, earlier)
    send(bb.at[0], bb.at[2], b_dn, t_dn, earlier)

    w_up, w_dn, wx_up, wx_dn = channel(5), channel(5), channel(), channel()

    def weight_to_x(zz):
        send(wb.at[x, :, zz], wb.at[x, :, zz], wx_up, x_up)
        send(wb.at[x, :, zz], wb.at[x, :, zz], wx_dn, x_dn)

    arrive(wb.at[x, 1 - y, z], w_y)
    wx_send = []

    def weight_x(zz, n):
        cu = copy(wb.at[x, :, zz], wb.at[x, :, zz], wx_up, x_up)
        cd = copy(wb.at[x, :, zz], wb.at[x, :, zz], wx_dn, x_dn)
        cu.start()
        cd.start()

    send(wb.at[x, :, z], wb.at[x, :, z], w_up + 1, z_up)
    send(wb.at[x, :, z], wb.at[x, :, z], w_dn + 1, z_dn)
    weight_x(z, 0)

    crossing = z // 4 == x % 2
    e_ch = channel(6)
    for i in range(1, 4):
        below, above = base + (z + 8 - i) % 8, base + (z + i) % 8
        zb, za = (z + 8 - i) % 8, (z + i) % 8
        arrive(kb.at[below], up_k + i)
        send(kb.at[below], kb.at[below], up_k + i + 1, z_up)
        if i == 3:
            up_edge = jnp.logical_and(crossing, w < 3)
            send(kb.at[below], kb.at[below], e_ch + 0, x_flip, up_edge)
        arrive(kb.at[above], dn_k + i)
        if i < 3:
            send(kb.at[above], kb.at[above], dn_k + i + 1, z_dn)
        else:
            dn_edge = jnp.logical_and(crossing, w > 0)
            send(kb.at[above], kb.at[above], e_ch + 2, x_flip, dn_edge)
        arrive(vb.at[below], up_v + i)
        if i < 3:
            send(vb.at[below], vb.at[below], up_v + i + 1, z_up)
        else:
            send(vb.at[below], vb.at[below], e_ch + 1, x_flip, up_edge)
        arrive(vb.at[above], dn_v + i)
        send(vb.at[above], vb.at[above], dn_v + i + 1, z_dn)
        if i == 3:
            send(vb.at[above], vb.at[above], e_ch + 3, x_flip, dn_edge)
        arrive(wb.at[x, :, zb], w_up + i)
        if i < 3:
            send(wb.at[x, :, zb], wb.at[x, :, zb], w_up + i + 1, z_up)
        else:
            send(wb.at[x, 0, zb], wb.at[x, 0, zb], w_up + i + 1, z_up)
        arrive(wb.at[x, :, za], w_dn + i)
        if i < 3:
            send(wb.at[x, :, za], wb.at[x, :, za], w_dn + i + 1, z_dn)
        else:
            send(wb.at[x, 1, za], wb.at[x, 1, za], w_dn + i + 1, z_dn)
        weight_x(zb, i)
        weight_x(za, i)
    zf = (z + 4) % 8
    far = base + zf
    arrive(kb.at[far], up_k + 4)
    send(kb.at[far], kb.at[far], e_ch + 4, x_flip, crossing)
    arrive(vb.at[far], dn_v + 4)
    send(vb.at[far], vb.at[far], e_ch + 5, x_flip, crossing)
    arrive(wb.at[x, 0, zf], w_up + 4)
    arrive(wb.at[x, 1, zf], w_dn + 4)
    weight_x(zf, 4)

    arrive(qb.at[1], q_up, earlier)
    arrive(bb.at[1], b_up, earlier)
    arrive(qb.at[2], q_dn, later)
    arrive(bb.at[2], b_dn, later)

    facing = z // 4 != x % 2
    over = 8 - base + z
    fz = 8 - base + (z + 4) % 8
    up_face = jnp.logical_and(facing, w < 3)
    dn_face = jnp.logical_and(facing, w > 0)
    f_up = 8 - base + (z + 5) % 8
    f_dn = 8 - base + (z + 3) % 8
    arrive(kb.at[f_up], e_ch + 0, up_face)
    arrive(vb.at[f_up], e_ch + 1, up_face)
    arrive(kb.at[f_dn], e_ch + 2, dn_face)
    arrive(vb.at[f_dn], e_ch + 3, dn_face)
    arrive(kb.at[fz], e_ch + 4, facing)
    arrive(vb.at[fz], e_ch + 5, facing)

    h_at = [h - (h + 3) // 4, h, h + 1 - h // 3]
    w_at = [w - (w + 3) // 4, w, w + 1 - w // 3]
    slots = [h_at[n // 3] * 4 + w_at[n % 3] for n in range(9)]
    lane = lax.broadcasted_iota(jnp.int32, (TILE, HD), 1)

    def unit(i, a):
        first = (9, 18, 0)[i]
        cols = pl.ds(pl.multiple_of(a * HD, HD), HD)
        q = qb[i, :, cols]
        m = jnp.full((TILE, HD), NEG, jnp.float32)
        for n in range(9):
            sc = lax.dot_general(q, kb[slots[n], :, cols], (((1,), (1,)), ((), ())),
                                 preferred_element_type=jnp.float32)
            sb[n] = sc
            m = jnp.maximum(m, jnp.maximum(sc[:, :HD], sc[:, HD:]) - bb[i, first + n : first + n + 1, :])
        m = jnp.max(m, axis=1, keepdims=True) * SCALE
        ones = jnp.ones((TILE, HD), jnp.bfloat16)
        acc = jnp.zeros((TILE, 2 * HD), jnp.float32)
        for n in range(9):
            shift = m + bb[i, first + n : first + n + 1, :]
            p = jnp.exp2(sb[n] * SCALE - jnp.concatenate([shift, shift], axis=1))
            v = jnp.concatenate([vb[slots[n], :, cols], ones], axis=1)
            acc = acc + jnp.dot(p.astype(jnp.bfloat16), v, preferred_element_type=jnp.float32)
        return m, acc

    po_ch, ps_ch = channel(6), channel(6)
    a_ch, c_ch = channel(9), channel(12)
    edge = ((1, earlier, t_dn), (2, later, t_up))

    def missing(k, cond):
        @pl.when(cond)
        def _():
            rs[k] = jnp.full((HEADS_DEV, 8, TILE), NEG, jnp.float32)
            ro[k] = jnp.zeros((HEADS_DEV, TILE, HD), jnp.bfloat16)

    missing(0, t == 0)
    missing(1, t == 3)

    def back(k, a, dev):
        return (copy(po.at[k, a], ro.at[1 - k, a], po_ch + 3 * k + a, dev),
                copy(ps.at[k, a], rs.at[1 - k, a], ps_ch + 3 * k + a, dev))

    def feature(gg, a):
        return ab.at[:, pl.ds(pl.multiple_of(gg * WIDTH + a * HD, HD), HD)]

    def remote_units(a):
        for i, cond, dev in edge:
            @pl.when(cond)
            def _(i=i, dev=dev):
                m, acc = unit(i, a)
                k = i - 1
                po[k, a] = acc[:, :HD].astype(jnp.bfloat16)
                stat = jnp.where(lane == 0, m, acc[:, HD:])
                ps[k, a] = stat.T[:8]
                for c in back(k, a, dev):
                    c.start()

    def own_unit(a):
        m, acc = unit(0, a)
        lo[...] = acc
        ls[...] = jnp.broadcast_to(m, (TILE, HD))

    def share(gg, a, ch, dev):
        return copy(feature(gg, a), feature(gg, a), ch, dev)

    def finish(a):
        for k, cond in ((0, earlier), (1, later)):
            @pl.when(cond)
            def _(k=k):
                copy(ro.at[k, a], ro.at[k, a], po_ch + 3 * (1 - k) + a, t_up).wait_recv()
                copy(rs.at[k, a], rs.at[k, a], ps_ch + 3 * (1 - k) + a, t_up).wait_recv()
        m0, num0, den0 = ls[...][:, :1], lo[:, :HD], lo[:, HD:]
        stats = []
        for k in range(2):
            r = rs[k, a]
            st = jnp.concatenate([r] * 16, axis=0).T
            stats.append((st[:, :1], st[:, 1:2]))
        top = jnp.maximum(m0, jnp.maximum(stats[0][0], stats[1][0]))
        f0 = jnp.exp2(m0 - top)
        num, den = num0 * f0, den0 * f0
        for k in range(2):
            mk, lk = stats[k]
            f = jnp.exp2(mk - top)
            num = num + ro[k, a].astype(jnp.float32) * f
            den = den + jnp.maximum(lk, 0.0) * f
        feature(g, a)[...] = (num / den).astype(jnp.bfloat16)
        for d in range(1, 4):
            share(g, a, a_ch + 3 * (d - 1) + a, peer(2 * d)).start()
        share(g, a, c_ch + a, partner).start()

    def head_step(a, _):
        remote_units(a)

        @pl.when(a > 0)
        def _():
            finish(a - 1)

        own_unit(a)
        return 0

    lax.fori_loop(0, 1, head_step, 0)
    xl, xr = (x + 3) % 4, (x + 1) % 4
    xf = (x + 2) % 4
    w2_up, w2_dn = channel(), channel()
    arrive(wb.at[xl], wx_up)
    send(wb.at[xl, 0], wb.at[xl, 0], w2_up, x_up)
    arrive(wb.at[xr], wx_dn)
    send(wb.at[xr, 1], wb.at[xr, 1], w2_dn, x_dn)
    lax.fori_loop(1, HEADS_DEV, head_step, 0)
    finish(HEADS_DEV - 1)

    for a in range(HEADS_DEV):
        for d in range(1, 4):
            src = (g + GROUPS - 2 * d) % GROUPS
            copy(feature(src, a), feature(src, a), a_ch + 3 * (d - 1) + a, z_up).wait_recv()
            share(src, a, c_ch + 3 * d + a, partner).start()
    arrive(wb.at[xf, 0], w2_up)
    arrive(wb.at[xf, 1], w2_dn)
    for a in range(HEADS_DEV):
        for d in range(4):
            src = (g + 1 - 2 * core + GROUPS - 2 * d) % GROUPS
            copy(feature(src, a), feature(src, a), c_ch + 3 * d + a, z_up).wait_recv()

    for n in range(3):
        cols = slice(n * 256, n * 256 + 256)
        acc = jnp.zeros((TILE, 256), jnp.float32)
        for j in range(GROUPS):
            rows = wb[j % 4, j // 4, :, :, cols].reshape(WIDTH, 256)
            acc = acc + jnp.dot(ab[:, j * WIDTH : (j + 1) * WIDTH], rows, preferred_element_type=jnp.float32)
        out_ref[:, cols] = acc.astype(jnp.bfloat16)

    for c, cond in sent:
        if cond is None:
            c.wait_send()
        else:
            pl.when(cond)(c.wait_send)
    copy(wb.at[x], wb.at[x], wx_up, x_up).wait_send()
    copy(wb.at[x], wb.at[x], wx_dn, x_dn).wait_send()
    for a in range(HEADS_DEV):
        for i, cond, dev in edge:
            for c in back(i - 1, a, dev):
                pl.when(cond)(c.wait_send)
        for d in range(1, 4):
            share(g, a, a_ch + 3 * (d - 1) + a, peer(2 * d)).wait_send()
        for d in range(4):
            share(g, a, c_ch + 3 * d + a, partner).wait_send()
    assert channels[0] <= N_CH


def local(queries, keys, values, window, out_weight):
    listed = jnp.where(window[0] >= 0, 0.0, BIG).astype(jnp.float32)
    bias = jnp.broadcast_to(jnp.pad(listed, (0, 5))[:, None], (32, HD))
    any_spec = pl.BlockSpec(memory_space=pl.ANY)
    bf16, f32 = jnp.bfloat16, jnp.float32
    return pl.pallas_call(
        kernel,
        out_shape=jax.ShapeDtypeStruct((TILE, out_weight.shape[1]), bf16),
        in_specs=[any_spec] * 5,
        out_specs=pl.BlockSpec(memory_space=pltpu.VMEM),
        scratch_shapes=[
            pltpu.VMEM((16, TILE, WIDTH), bf16),
            pltpu.VMEM((16, TILE, WIDTH), bf16),
            pltpu.VMEM((4, 2, 8, 48, 768), bf16),
            pltpu.VMEM((3, TILE, WIDTH), bf16),
            pltpu.VMEM((3, 32, HD), f32),
            pltpu.VMEM((TILE, GROUPS * WIDTH), bf16),
            pltpu.VMEM((9, TILE, TILE), f32),
            pltpu.VMEM((2, HEADS_DEV, TILE, HD), bf16),
            pltpu.VMEM((2, HEADS_DEV, 8, TILE), f32),
            pltpu.VMEM((2, HEADS_DEV, TILE, HD), bf16),
            pltpu.VMEM((2, HEADS_DEV, 8, TILE), f32),
            pltpu.VMEM((TILE, 2 * HD), f32),
            pltpu.VMEM((TILE, HD), f32),
            pltpu.SemaphoreType.DMA((N_CH,)),
            pltpu.SemaphoreType.DMA((N_CH,)),
            pltpu.SemaphoreType.DMA((5,)),
        ],
        compiler_params=pltpu.CompilerParams(
            collective_id=0, has_side_effects=True, vmem_limit_bytes=60 * 1024 * 1024),
    )(queries, keys, values, bias, out_weight)


def solution(mesh):
    in_specs = (
        P(("seq", "head"), None),
        P("seq", "head"),
        P("seq", "head"),
        P("seq", None),
        P("seq", "head"),
    )
    return jax.shard_map(local, mesh=mesh, in_specs=in_specs, out_specs=P("seq", "head"), check_vma=False)
```

time: 857 us -> 122 us (0.14)
  the two profiles are of different devices: /device:TPU:40 before, /device:TPU:329 now
where the time goes in v1:
time: 122 us
  Pallas kernels  119 us (98%)
  local copies, waits for them, and re-layouts  2.45 us (2%)
    pallas_call x1, Pallas kernels, local(): pl.pallas_call(kernel, out_shape=jax.ShapeDtypeStruct((TILE, out_weight.s...  119 us

profile of v1, /device:TPU:329, one launch (start us, length us, event | category | flops | bytes accessed | tf_op | source)
XLA Modules:
  0.0 122.1 jit_solution(17905219589497217343)
XLA Ops:
  0.0 0.7 fusion
  0.7 0.7 broadcast_in_dim.16.bias_in
  1.3 119.0 %shard_map.55 = bf16[256,768]{1,0:T(8,128)(2,1)} custom-call(bf16[32,3072]{1,0:T(8,128)(2,1)} %q_in.1, bf16[256,384]{1,0:T(8,128)(2,1)} %k_in.1, bf16[256,384]{1,0:T(8,128)(2,1)} %v_in.1, f32[32,128]{1,0:T(8,128)} %broadcast_in_dim.16.bias_in, bf16[48,768]{1,0:T(8,128)(2,1)} %w_in.1), custom_call_target="tpu_custom_call" | custom-call | tf_op jit(solution)/shard_map/pallas_call | solution.py:360
  120.3 1.8 %copy.7 = bf16[256,768]{1,0:T(8,128)(2,1)} copy(bf16[256,768]{1,0:T(8,128)(2,1)} %shard_map.55) | data formatting | bytes 786432
  (1 shorter events, 0.0 us)

commit v2 on v1

v2 whole, which is shorter than its diff:
```python
import functools

import jax
import jax.numpy as jnp
from jax import lax
from jax.experimental import pallas as pl
from jax.experimental.pallas import tpu as pltpu
from jax.sharding import PartitionSpec as P

MESH = pl.DeviceIdType.MESH
TILE = 256
HD = 128
HEADS_DEV = 3
WIDTH = HD * HEADS_DEV
GROUPS = 8
NEG = -1e30
BIG = 1e30
SCALE = 1.4426950408889634 * HD**-0.5
N_CH = 200


def kernel(q_in, k_in, v_in, win, w_in, out_ref,
           kv, wb, qb, bb, ab, sb, po, ps, ro, rs, lo, ls, send_sem, recv_sem, loc_sem):
    s = lax.axis_index("seq")
    g = lax.axis_index("head")
    y = s // 32
    x = (s // 8) % 4
    z = s % 8
    t = 2 * y + x // 2
    h = 2 * (x % 2) + z // 4
    w = z % 4
    core = g % 2

    def at(yy, xx, zz):
        return (yy * 32 + xx * 8 + zz, g)

    def at_time(tt):
        return (16 * tt + s % 16, g)

    z_up, z_dn = at(y, x, (z + 1) % 8), at(y, x, (z + 7) % 8)
    x_up, x_dn = at(y, (x + 1) % 4, z), at(y, (x + 3) % 4, z)
    x_flip = at(y, x + 1 - 2 * (x % 2), z)
    y_flip = at(1 - y, x, z)
    t_up, t_dn = at_time((t + 1) % 4), at_time((t + 3) % 4)
    partner = (s, g + 1 - 2 * core)

    def peer(d):
        return (s, (g + d) % GROUPS)

    barrier = pltpu.get_barrier_semaphore()
    greeted = [z_up, z_dn, x_up, x_dn, y_flip, t_up, t_dn] + [peer(d) for d in range(1, GROUPS)]
    for other in greeted:
        pl.semaphore_signal(barrier, inc=1, device_id=other, device_id_type=MESH)

    channels = [0]
    draining = [False]
    done = {}

    def channel(n=1):
        channels[0] += n
        return channels[0] - n

    def copy(src, dst, ch, dev):
        return pltpu.make_async_remote_copy(
            src_ref=src, dst_ref=dst, send_sem=send_sem.at[ch], recv_sem=recv_sem.at[ch],
            device_id=dev, device_id_type=MESH)

    def send(ref, ch, dev, cond=None, dst=None):
        c = copy(ref, ref if dst is None else dst, ch, dev)
        act = c.wait_send if draining[0] else c.start
        if cond is None:
            act()
        else:
            pl.when(cond)(act)

    def do(step, *which):
        step(*which)
        done[step, which] = None

    def arrive(dst, ch, cond=None):
        if draining[0]:
            return
        c = copy(dst, dst, ch, z_up)
        if cond is None:
            c.wait_recv()
        else:
            pl.when(cond)(c.wait_recv)

    base = 8 * (x % 2)
    own = base + z
    row0 = pl.multiple_of(g * 32, 32)
    col0 = pl.multiple_of(g * WIDTH, HD)
    local = []
    for a in range(HEADS_DEV):
        cols = pl.ds(a * HD, HD)
        local.append(pltpu.make_async_copy(k_in.at[:, cols], kv.at[own, a, 0], loc_sem.at[2 * a]))
        local.append(pltpu.make_async_copy(v_in.at[:, cols], kv.at[own, a, 1], loc_sem.at[2 * a + 1]))
    for p in range(2):
        local.append(pltpu.make_async_copy(w_in.at[:, pl.ds(p * WIDTH, WIDTH)], wb.at[p, x, y, z], loc_sem.at[6 + p]))
    local.append(pltpu.make_async_copy(q_in.at[:, pl.ds(col0, WIDTH)], qb.at[0, pl.ds(row0, 32)], loc_sem.at[8]))
    for c in local:
        c.start()
    for n in range(27):
        bb[0, n : n + 1, :] = jnp.full((1, HD), jnp.where(win[0, n] >= 0, 0.0, BIG), jnp.float32)
    for c in local:
        c.wait()
    pl.semaphore_wait(barrier, len(greeted))

    up, dn = channel(15), channel(15)
    e_ch = channel(9)
    q_ch = channel(GROUPS)
    w_y = channel()
    w_up, w_dn = channel(10), channel(10)
    x_up_ch, x_dn_ch, x2_ch = channel(16), channel(16), channel(16)
    wy_ch = channel(4)
    later, earlier = t < 3, t > 0

    def own_block(a):
        send(kv.at[own, a], up + 3 + a, z_up)
        send(kv.at[own, a], dn + 3 + a, z_dn)

    crossing = z // 4 == x % 2
    up_edge = jnp.logical_and(crossing, w < 3)
    dn_edge = jnp.logical_and(crossing, w > 0)

    def ring(i, a):
        below, above = base + (z + 8 - i) % 8, base + (z + i) % 8
        if i == 4:
            arrive(kv.at[below, a, 0], up + 3 * i + a)
            arrive(kv.at[below, a, 1], dn + 3 * i + a)
            send(kv.at[below, a], e_ch + a, x_flip, crossing)
            return
        arrive(kv.at[below, a], up + 3 * i + a)
        if i < 3:
            send(kv.at[below, a], up + 3 * i + 3 + a, z_up)
        else:
            send(kv.at[below, a, 0], up + 3 * i + 3 + a, z_up)
            send(kv.at[below, a], e_ch + 3 + a, x_flip, up_edge)
        arrive(kv.at[above, a], dn + 3 * i + a)
        if i < 3:
            send(kv.at[above, a], dn + 3 * i + 3 + a, z_dn)
        else:
            send(kv.at[above, a, 1], dn + 3 * i + 3 + a, z_dn)
            send(kv.at[above, a], e_ch + 6 + a, x_flip, dn_edge)

    def z_of(n):
        return (z + 8 - (n + 1) // 2) % 8 if n % 2 else (z + n // 2) % 8

    def part(p, xx, zz):
        return wb.at[0, xx, :, zz] if p == 0 else wb.at[1, xx, y, zz]

    def weight_x(n):
        for p in range(2):
            send(part(p, x, z_of(n)), x_up_ch + 2 * n + p, x_up)
            send(part(p, x, z_of(n)), x_dn_ch + 2 * n + p, x_dn)

    def weight_z(i):
        zb, za = (z + 8 - i) % 8, (z + i) % 8
        for p in range(2):
            if i == 0:
                send(part(p, x, z), w_up + p, z_up)
                send(part(p, x, z), w_dn + p, z_dn)
                continue
            if i == 4:
                continue
            arrive(part(p, x, zb), w_up + 2 * i - 2 + p)
            arrive(part(p, x, za), w_dn + 2 * i - 2 + p)
            if i < 3:
                send(part(p, x, zb), w_up + 2 * i + p, z_up)
                send(part(p, x, za), w_dn + 2 * i + p, z_dn)
            elif p == 0:
                send(wb.at[0, x, 0, zb], w_up + 6, z_up)
                send(wb.at[0, x, 1, za], w_dn + 6, z_dn)
            else:
                send(part(1, x, zb), w_up + 7, z_up)
        if i == 0:
            weight_x(0)
        elif i < 4:
            weight_x(2 * i - 1)
            weight_x(2 * i)
        else:
            arrive(wb.at[0, x, 0, zb], w_up + 6)
            arrive(wb.at[0, x, 1, za], w_dn + 6)
            arrive(part(1, x, zb), w_up + 7)
            weight_x(7)

    xl, xr, xf = (x + 3) % 4, (x + 1) % 4, (x + 2) % 4
    low = z < 4

    def weight_x2(n):
        for p in range(2):
            arrive(part(p, xl, z_of(n)), x_up_ch + 2 * n + p)
            arrive(part(p, xr, z_of(n)), x_dn_ch + 2 * n + p)
            send(part(p, xl, z_of(n)), x2_ch + 2 * n + p, x_up, z >= 4)
            send(part(p, xr, z_of(n)), x2_ch + 2 * n + p, x_dn, low)

    def weight_y():
        for n, xx in enumerate((x, xl, xr)):
            send(wb.at[1, xx, y], wy_ch + n, y_flip)

    def weight_y2():
        for n in range(8):
            for p in range(2):
                arrive(part(p, xf, z_of(n)), x2_ch + 2 * n + p)
        send(wb.at[1, xf, y], wy_ch + 3, y_flip)

    qt = channel(4)

    def query_out():
        for d in range(1, GROUPS):
            col = pl.multiple_of(((g + d) % GROUPS) * WIDTH, HD)
            send(q_in.at[:, pl.ds(col, WIDTH)], q_ch + d, peer(d), dst=qb.at[0, pl.ds(row0, 32)])

    def query_time():
        for d in range(1, GROUPS):
            src_row = pl.multiple_of(((g + GROUPS - d) % GROUPS) * 32, 32)
            arrive(qb.at[0, pl.ds(src_row, 32)], q_ch + d)
        send(qb.at[0], qt, t_up, later, dst=qb.at[1])
        send(bb.at[0], qt + 1, t_up, later, dst=bb.at[1])
        send(qb.at[0], qt + 2, t_dn, earlier, dst=qb.at[2])
        send(bb.at[0], qt + 3, t_dn, earlier, dst=bb.at[2])

    def weight_pair():
        send(wb.at[0, x, y, z], w_y, y_flip)

    do(own_block, 0)
    do(query_out)
    do(weight_pair)
    do(own_block, 1)
    do(ring, 1, 0)
    arrive(wb.at[0, x, 1 - y, z], w_y)
    do(weight_z, 0)
    do(own_block, 2)
    do(ring, 2, 0)
    do(query_time)
    do(ring, 1, 1)
    do(weight_z, 1)
    do(ring, 3, 0)
    do(ring, 2, 1)
    do(weight_z, 2)
    do(ring, 4, 0)
    do(ring, 1, 2)
    do(weight_z, 3)
    do(ring, 3, 1)
    do(ring, 2, 2)
    do(weight_x2, 0)
    do(weight_x2, 1)
    do(weight_x2, 2)
    do(weight_z, 4)
    do(ring, 4, 1)

    h_at = [h - (h + 3) // 4, h, h + 1 - h // 3]
    w_at = [w - (w + 3) // 4, w, w + 1 - w // 3]
    slots = [h_at[n // 3] * 4 + w_at[n % 3] for n in range(9)]
    lane = lax.broadcasted_iota(jnp.int32, (TILE, HD), 1)

    def unit(i, a):
        first = (9, 18, 0)[i]
        q = qb[i, :, pl.ds(pl.multiple_of(a * HD, HD), HD)]
        m = jnp.full((TILE, HD), NEG, jnp.float32)
        for n in range(9):
            sc = lax.dot_general(q, kv[slots[n], a, 0], (((1,), (1,)), ((), ())),
                                 preferred_element_type=jnp.float32)
            sb[n] = sc
            m = jnp.maximum(m, jnp.maximum(sc[:, :HD], sc[:, HD:]) - bb[i, first + n : first + n + 1, :])
        m = jnp.max(m, axis=1, keepdims=True) * SCALE
        ones = jnp.ones((TILE, HD), jnp.bfloat16)
        acc = jnp.zeros((TILE, 2 * HD), jnp.float32)
        for n in range(9):
            shift = m + bb[i, first + n : first + n + 1, :]
            p = jnp.exp2(sb[n] * SCALE - jnp.concatenate([shift, shift], axis=1))
            v = jnp.concatenate([kv[slots[n], a, 1], ones], axis=1)
            acc = acc + jnp.dot(p.astype(jnp.bfloat16), v, preferred_element_type=jnp.float32)
        return m, acc

    po_ch, ps_ch = channel(6), channel(6)
    a_ch, c_ch = channel(9), channel(12)
    edge = ((1, earlier, t_dn), (2, later, t_up))

    def missing(k, cond):
        @pl.when(cond)
        def _():
            rs[k] = jnp.full((HEADS_DEV, 8, TILE), NEG, jnp.float32)
            ro[k] = jnp.zeros((HEADS_DEV, TILE, HD), jnp.bfloat16)

    missing(0, t == 0)
    missing(1, t == 3)

    def back(k, a, dev):
        return (copy(po.at[k, a], ro.at[1 - k, a], po_ch + 3 * k + a, dev),
                copy(ps.at[k, a], rs.at[1 - k, a], ps_ch + 3 * k + a, dev))

    def feature(gg, a):
        return ab.at[:, pl.ds(pl.multiple_of(gg * WIDTH + a * HD, HD), HD)]

    def remote_unit(j, a):
        i, cond, dev = edge[j]

        @pl.when(cond)
        def _():
            m, acc = unit(i, a)
            k = i - 1
            po[k, a] = acc[:, :HD].astype(jnp.bfloat16)
            stat = jnp.where(lane == 0, m, acc[:, HD:])
            ps[k, a] = stat.T[:8]
            for c in back(k, a, dev):
                c.start()

    def own_unit(a):
        m, acc = unit(0, a)
        lo[a % 2] = acc
        ls[a % 2] = jnp.broadcast_to(m, (TILE, HD))

    def share(gg, a, ch, dev):
        return copy(feature(gg, a), feature(gg, a), ch, dev)

    def finish(a):
        for k, cond in ((0, earlier), (1, later)):
            @pl.when(cond)
            def _(k=k):
                copy(ro.at[k, a], ro.at[k, a], po_ch + 3 * (1 - k) + a, t_up).wait_recv()
                copy(rs.at[k, a], rs.at[k, a], ps_ch + 3 * (1 - k) + a, t_up).wait_recv()
        m0, num0, den0 = ls[a % 2][:, :1], lo[a % 2, :, :HD], lo[a % 2, :, HD:]
        stats = []
        for k in range(2):
            r = rs[k, a]
            st = jnp.concatenate([r] * 16, axis=0).T
            stats.append((st[:, :1], st[:, 1:2]))
        top = jnp.maximum(m0, jnp.maximum(stats[0][0], stats[1][0]))
        f0 = jnp.exp2(m0 - top)
        num, den = num0 * f0, den0 * f0
        for k in range(2):
            mk, lk = stats[k]
            f = jnp.exp2(mk - top)
            num = num + ro[k, a].astype(jnp.float32) * f
            den = den + jnp.maximum(lk, 0.0) * f
        feature(g, a)[...] = (num / den).astype(jnp.bfloat16)
        for d in range(1, 4):
            share(g, a, a_ch + 3 * (d - 1) + a, peer(2 * d)).start()
        share(g, a, c_ch + a, partner).start()

    def relay(a):
        for d in range(1, 4):
            src = (g + GROUPS - 2 * d) % GROUPS
            copy(feature(src, a), feature(src, a), a_ch + 3 * (d - 1) + a, z_up).wait_recv()
            share(src, a, c_ch + 3 * d + a, partner).start()

    arrive(qb.at[1], qt, earlier)
    arrive(bb.at[1], qt + 1, earlier)
    arrive(qb.at[2], qt + 2, later)
    arrive(bb.at[2], qt + 3, later)

    facing = z // 4 != x % 2
    up_face = jnp.logical_and(facing, w < 3)
    dn_face = jnp.logical_and(facing, w > 0)

    def crossed(a):
        arrive(kv.at[8 - base + (z + 5) % 8, a], e_ch + 3 + a, up_face)
        arrive(kv.at[8 - base + (z + 3) % 8, a], e_ch + 6 + a, dn_face)
        arrive(kv.at[8 - base + (z + 4) % 8, a], e_ch + a, facing)

    def head_step(a, _):
        crossed(a)
        remote_unit(0, a)

        @pl.when(a == 0)
        def _():
            do(ring, 3, 2)

        remote_unit(1, a)

        @pl.when(a == 0)
        def _():
            do(ring, 4, 2)

        @pl.when(a > 0)
        def _():
            finish(a - 1)

        @pl.when(a == 1)
        def _():
            for n in range(3, 8):
                do(weight_x2, n)
            do(weight_y)

        own_unit(a)

        @pl.when(a == 2)
        def _():
            relay(0)
            do(weight_y2)

        return 0

    lax.fori_loop(0, HEADS_DEV, head_step, 0)
    finish(HEADS_DEV - 1)
    relay(1)
    for n, xx in enumerate((x, xl, xr, xf)):
        arrive(wb.at[1, xx, 1 - y], wy_ch + n)
    relay(2)
    for a in range(HEADS_DEV):
        for d in range(4):
            src = (g + 1 - 2 * core + GROUPS - 2 * d) % GROUPS
            copy(feature(src, a), feature(src, a), c_ch + 3 * d + a, z_up).wait_recv()

    for n in range(3):
        acc = jnp.zeros((TILE, 256), jnp.float32)
        for j in range(GROUPS):
            if n == 1:
                rows = jnp.concatenate([wb[0, j % 4, j // 4, :, :, 256:], wb[1, j % 4, j // 4, :, :, :128]], axis=2)
            else:
                rows = wb[n // 2, j % 4, j // 4, :, :, (0, 0, 128)[n] : (256, 0, 384)[n]]
            acc = acc + jnp.dot(ab[:, j * WIDTH : (j + 1) * WIDTH], rows.reshape(WIDTH, 256),
                                preferred_element_type=jnp.float32)
        out_ref[:, n * 256 : n * 256 + 256] = acc.astype(jnp.bfloat16)

    draining[0] = True
    for step, which in done:
        step(*which)
    for a in range(HEADS_DEV):
        for i, cond, dev in edge:
            for c in back(i - 1, a, dev):
                pl.when(cond)(c.wait_send)
        for d in range(1, 4):
            share(g, a, a_ch + 3 * (d - 1) + a, peer(2 * d)).wait_send()
        for d in range(4):
            share(g, a, c_ch + 3 * d + a, partner).wait_send()
    assert channels[0] <= N_CH


def local(queries, keys, values, window, out_weight):
    any_spec = pl.BlockSpec(memory_space=pl.ANY)
    bf16, f32 = jnp.bfloat16, jnp.float32
    return pl.pallas_call(
        kernel,
        out_shape=jax.ShapeDtypeStruct((TILE, out_weight.shape[1]), bf16),
        in_specs=[any_spec] * 3 + [pl.BlockSpec(memory_space=pltpu.SMEM), any_spec],
        out_specs=pl.BlockSpec(memory_space=pltpu.VMEM),
        scratch_shapes=[
            pltpu.VMEM((16, HEADS_DEV, 2, TILE, HD), bf16),
            pltpu.VMEM((2, 4, 2, 8, 48, WIDTH), bf16),
            pltpu.VMEM((3, TILE, WIDTH), bf16),
            pltpu.VMEM((3, 32, HD), f32),
            pltpu.VMEM((TILE, GROUPS * WIDTH), bf16),
            pltpu.VMEM((9, TILE, TILE), f32),
            pltpu.VMEM((2, HEADS_DEV, TILE, HD), bf16),
            pltpu.VMEM((2, HEADS_DEV, 8, TILE), f32),
            pltpu.VMEM((2, HEADS_DEV, TILE, HD), bf16),
            pltpu.VMEM((2, HEADS_DEV, 8, TILE), f32),
            pltpu.VMEM((2, TILE, 2 * HD), f32),
            pltpu.VMEM((2, TILE, HD), f32),
            pltpu.SemaphoreType.DMA((N_CH,)),
            pltpu.SemaphoreType.DMA((N_CH,)),
            pltpu.SemaphoreType.DMA((9,)),
        ],
        compiler_params=pltpu.CompilerParams(
            collective_id=0, has_side_effects=True, vmem_limit_bytes=60 * 1024 * 1024),
    )(queries, keys, values, window, out_weight)


def solution(mesh):
    in_specs = (
        P(("seq", "head"), None),
        P("seq", "head"),
        P("seq", "head"),
        P("seq", None),
        P("seq", "head"),
    )
    return jax.shard_map(local, mesh=mesh, in_specs=in_specs, out_specs=P("seq", "head"), check_vma=False)
```

time: 122 us -> 128 us (1.049)
  the two profiles are of different devices: /device:TPU:329 before, /device:TPU:69 now
where the time goes in v2:
time: 128 us
  Pallas kernels  126 us (98%)
  local copies, waits for them, and re-layouts  1.77 us (1%)
    pallas_call x1, Pallas kernels, local(): pl.pallas_call(kernel, out_shape=jax.ShapeDtypeStruct((TILE, out_weight.s...  126 us

profile of v2, /device:TPU:69, one launch (start us, length us, event | category | flops | bytes accessed | tf_op | source)
XLA Modules:
  0.0 127.6 jit_solution(6319852085088526757)
XLA Ops:
  0.0 125.8 %shard_map.55 = bf16[256,768]{1,0:T(8,128)(2,1)} custom-call(bf16[32,3072]{1,0:T(8,128)(2,1)} %q_in.1, bf16[256,384]{1,0:T(8,128)(2,1)} %k_in.1, bf16[256,384]{1,0:T(8,128)(2,1)} %v_in.1, s32[1,27]{1,0:T(1,128)} %win.1, bf16[48,768]{1,0:T(8,128)(2,1)} %w_in.1), custom_call_target="tpu_custom_call" | custom-call | tf_op jit(solution)/shard_map/pallas_call | solution.py:434
  125.8 1.8 %copy.7 = bf16[256,768]{1,0:T(8,128)(2,1)} copy(bf16[256,768]{1,0:T(8,128)(2,1)} %shard_map.55) | data formatting | bytes 786432

commit v3 on v2

--- a/solution.py
+++ b/solution.py
@@ -194,15 +194,13 @@
             send(part(p, xl, z_of(n)), x2_ch + 2 * n + p, x_up, z >= 4)
             send(part(p, xr, z_of(n)), x2_ch + 2 * n + p, x_dn, low)
 
-    def weight_y():
-        for n, xx in enumerate((x, xl, xr)):
-            send(wb.at[1, xx, y], wy_ch + n, y_flip)
-
-    def weight_y2():
-        for n in range(8):
-            for p in range(2):
-                arrive(part(p, xf, z_of(n)), x2_ch + 2 * n + p)
-        send(wb.at[1, xf, y], wy_ch + 3, y_flip)
+    def weight_y(n):
+        xx = (x, xl, xr, xf)[n]
+        if n == 3:
+            for m in range(8):
+                for p in range(2):
+                    arrive(part(p, xf, z_of(m)), x2_ch + 2 * m + p)
+        send(wb.at[1, xx, y], wy_ch + n, y_flip)
 
     qt = channel(4)
 
@@ -223,31 +221,35 @@
     def weight_pair():
         send(wb.at[0, x, y, z], w_y, y_flip)
 
+    do(weight_pair)
     do(own_block, 0)
     do(query_out)
-    do(weight_pair)
-    do(own_block, 1)
-    do(ring, 1, 0)
     arrive(wb.at[0, x, 1 - y, z], w_y)
     do(weight_z, 0)
+    do(own_block, 1)
+    do(weight_z, 1)
+    do(ring, 1, 0)
+    do(query_time)
+    do(weight_z, 2)
+    do(weight_x2, 0)
+    do(ring, 2, 0)
+    do(weight_z, 3)
     do(own_block, 2)
-    do(ring, 2, 0)
-    do(query_time)
+    do(weight_x2, 1)
+    do(weight_x2, 2)
     do(ring, 1, 1)
-    do(weight_z, 1)
     do(ring, 3, 0)
+    do(weight_z, 4)
+    do(weight_y, 0)
+    do(ring, 1, 2)
+    do(weight_x2, 3)
+    do(weight_x2, 4)
     do(ring, 2, 1)
-    do(weight_z, 2)
     do(ring, 4, 0)
-    do(ring, 1, 2)
-    do(weight_z, 3)
+    do(weight_x2, 5)
+    do(weight_x2, 6)
     do(ring, 3, 1)
     do(ring, 2, 2)
-    do(weight_x2, 0)
-    do(weight_x2, 1)
-    do(weight_x2, 2)
-    do(weight_z, 4)
-    do(ring, 4, 1)
 
     h_at = [h - (h + 3) // 4, h, h + 1 - h // 3]
     w_at = [w - (w + 3) // 4, w, w + 1 - w // 3]
@@ -365,30 +367,34 @@
 
         @pl.when(a == 0)
         def _():
+            do(ring, 4, 1)
+
+        remote_unit(1, a)
+
+        @pl.when(a == 0)
+        def _():
             do(ring, 3, 2)
-
-        remote_unit(1, a)
+            do(weight_x2, 7)
+
+        @pl.when(a > 0)
+        def _():
+            finish(a - 1)
+
+        own_unit(a)
 
         @pl.when(a == 0)
         def _():
             do(ring, 4, 2)
-
-        @pl.when(a > 0)
-        def _():
-            finish(a - 1)
+            do(weight_y, 1)
+            do(weight_y, 2)
 
         @pl.when(a == 1)
         def _():
-            for n in range(3, 8):
-                do(weight_x2, n)
-            do(weight_y)
-
-        own_unit(a)
+            do(weight_y, 3)
 
         @pl.when(a == 2)
         def _():
             relay(0)
-            do(weight_y2)
 
         return 0
 

time: 128 us -> 111 us (0.87)
  the two profiles are of different devices: /device:TPU:69 before, /device:TPU:5 now
where the time goes in v3:
time: 111 us; the launch traced here: 110 us
  Pallas kernels  109 us (98%)
  local copies, waits for them, and re-layouts  1.77 us (2%)
    pallas_call x1, Pallas kernels, local(): pl.pallas_call(kernel, out_shape=jax.ShapeDtypeStruct((TILE, out_weight.s...  109 us

profile of v3, /device:TPU:5, one launch (start us, length us, event | category | flops | bytes accessed | tf_op | source)
XLA Modules:
  0.0 110.5 jit_solution(4332765826238553946)
XLA Ops:
  0.0 108.7 %shard_map.55 = bf16[256,768]{1,0:T(8,128)(2,1)} custom-call(bf16[32,3072]{1,0:T(8,128)(2,1)} %q_in.1, bf16[256,384]{1,0:T(8,128)(2,1)} %k_in.1, bf16[256,384]{1,0:T(8,128)(2,1)} %v_in.1, s32[1,27]{1,0:T(1,128)} %win.1, bf16[48,768]{1,0:T(8,128)(2,1)} %w_in.1), custom_call_target="tpu_custom_call" | custom-call | tf_op jit(solution)/shard_map/pallas_call | solution.py:440
  108.7 1.8 %copy.7 = bf16[256,768]{1,0:T(8,128)(2,1)} copy(bf16[256,768]{1,0:T(8,128)(2,1)} %shard_map.55) | data formatting | bytes 786432

commit v4 on v3

--- a/solution.py
+++ b/solution.py
@@ -16,11 +16,11 @@
 NEG = -1e30
 BIG = 1e30
 SCALE = 1.4426950408889634 * HD**-0.5
-N_CH = 200
+N_CH = 108
 
 
 def kernel(q_in, k_in, v_in, win, w_in, out_ref,
-           kv, wb, qb, bb, ab, sb, po, ps, ro, rs, lo, ls, send_sem, recv_sem, loc_sem):
+           kv, wb, w2, wf, qb, bb, ab, sb, po, ps, ro, rs, lo, ls, send_sem, recv_sem, loc_sem):
     s = lax.axis_index("seq")
     g = lax.axis_index("head")
     y = s // 32
@@ -95,8 +95,8 @@
         cols = pl.ds(a * HD, HD)
         local.append(pltpu.make_async_copy(k_in.at[:, cols], kv.at[own, a, 0], loc_sem.at[2 * a]))
         local.append(pltpu.make_async_copy(v_in.at[:, cols], kv.at[own, a, 1], loc_sem.at[2 * a + 1]))
-    for p in range(2):
-        local.append(pltpu.make_async_copy(w_in.at[:, pl.ds(p * WIDTH, WIDTH)], wb.at[p, x, y, z], loc_sem.at[6 + p]))
+    local.append(pltpu.make_async_copy(w_in.at[:, pl.ds(0, WIDTH)], wb.at[x, z, y], loc_sem.at[6]))
+    local.append(pltpu.make_async_copy(w_in.at[:, pl.ds(WIDTH, WIDTH)], w2.at[z, x], loc_sem.at[7]))
     local.append(pltpu.make_async_copy(q_in.at[:, pl.ds(col0, WIDTH)], qb.at[0, pl.ds(row0, 32)], loc_sem.at[8]))
     for c in local:
         c.start()
@@ -106,13 +106,14 @@
         c.wait()
     pl.semaphore_wait(barrier, len(greeted))
 
-    up, dn = channel(15), channel(15)
+    up, dn = channel(12) - 3, channel(12) - 3
     e_ch = channel(9)
-    q_ch = channel(GROUPS)
+    q_ch = channel()
     w_y = channel()
-    w_up, w_dn = channel(10), channel(10)
-    x_up_ch, x_dn_ch, x2_ch = channel(16), channel(16), channel(16)
-    wy_ch = channel(4)
+    w_up, w_dn = channel(4), channel(4)
+    x_up_ch, x_dn_ch, x2_ch = channel(8), channel(8), channel(8)
+    wy_ch, p_up, p_dn, p_x2 = channel(), channel(), channel(), channel()
+    pz_up, pz_dn = channel(4), channel(4)
     later, earlier = t < 3, t > 0
 
     def own_block(a):
@@ -125,107 +126,124 @@
 
     def ring(i, a):
         below, above = base + (z + 8 - i) % 8, base + (z + i) % 8
+        wb_, wa_ = (w + 8 - i) % 4, (w + i) % 4
         if i == 4:
-            arrive(kv.at[below, a, 0], up + 3 * i + a)
-            arrive(kv.at[below, a, 1], dn + 3 * i + a)
+            arrive(kv.at[below, a], up + 3 * i + a, w >= 2)
+            arrive(kv.at[below, a], dn + 3 * i + a, w < 2)
             send(kv.at[below, a], e_ch + a, x_flip, crossing)
             return
-        arrive(kv.at[below, a], up + 3 * i + a)
-        if i < 3:
-            send(kv.at[below, a], up + 3 * i + 3 + a, z_up)
-        else:
-            send(kv.at[below, a, 0], up + 3 * i + 3 + a, z_up)
+        arrive(kv.at[below, a], up + 3 * i + a, None if i == 1 else wb_ > 0)
+        send(kv.at[below, a], up + 3 * i + 3 + a, z_up, wb_ > (0 if i < 3 else 1))
+        if i == 3:
             send(kv.at[below, a], e_ch + 3 + a, x_flip, up_edge)
-        arrive(kv.at[above, a], dn + 3 * i + a)
-        if i < 3:
-            send(kv.at[above, a], dn + 3 * i + 3 + a, z_dn)
-        else:
-            send(kv.at[above, a, 1], dn + 3 * i + 3 + a, z_dn)
+        arrive(kv.at[above, a], dn + 3 * i + a, None if i == 1 else wa_ < 3)
+        send(kv.at[above, a], dn + 3 * i + 3 + a, z_dn, wa_ < (3 if i < 3 else 2))
+        if i == 3:
             send(kv.at[above, a], e_ch + 6 + a, x_flip, dn_edge)
 
     def z_of(n):
         return (z + 8 - (n + 1) // 2) % 8 if n % 2 else (z + n // 2) % 8
 
-    def part(p, xx, zz):
-        return wb.at[0, xx, :, zz] if p == 0 else wb.at[1, xx, y, zz]
+    xl, xr, xf = (x + 3) % 4, (x + 1) % 4, (x + 2) % 4
+
+    def start(src, dst, ch, dev):
+        if not draining[0]:
+            copy(src, dst, ch, dev).start()
+
+    def weight_y(n):
+        start(w2.at[z_of(n)], wf.at[z_of(n)], wy_ch, y_flip)
 
     def weight_x(n):
-        for p in range(2):
-            send(part(p, x, z_of(n)), x_up_ch + 2 * n + p, x_up)
-            send(part(p, x, z_of(n)), x_dn_ch + 2 * n + p, x_dn)
+        block = wb.at[x, z_of(n)]
+        send(block, x_up_ch + n, x_up)
+        send(block, x_dn_ch + n, x_dn)
 
     def weight_z(i):
-        zb, za = (z + 8 - i) % 8, (z + i) % 8
-        for p in range(2):
-            if i == 0:
-                send(part(p, x, z), w_up + p, z_up)
-                send(part(p, x, z), w_dn + p, z_dn)
-                continue
-            if i == 4:
-                continue
-            arrive(part(p, x, zb), w_up + 2 * i - 2 + p)
-            arrive(part(p, x, za), w_dn + 2 * i - 2 + p)
-            if i < 3:
-                send(part(p, x, zb), w_up + 2 * i + p, z_up)
-                send(part(p, x, za), w_dn + 2 * i + p, z_dn)
-            elif p == 0:
-                send(wb.at[0, x, 0, zb], w_up + 6, z_up)
-                send(wb.at[0, x, 1, za], w_dn + 6, z_dn)
-            else:
-                send(part(1, x, zb), w_up + 7, z_up)
         if i == 0:
+            send(wb.at[x, z], w_up, z_up)
+            send(wb.at[x, z], w_dn, z_dn)
             weight_x(0)
-        elif i < 4:
-            weight_x(2 * i - 1)
-            weight_x(2 * i)
+            return
+        below, above = wb.at[x, (z + 8 - i) % 8], wb.at[x, (z + i) % 8]
+        if i == 4:
+            arrive(below.at[0], w_up + 3)
+            arrive(below.at[1], w_dn + 3)
+            weight_x(7)
+            return
+        arrive(below, w_up + i - 1)
+        arrive(above, w_dn + i - 1)
+        if i < 3:
+            send(below, w_up + i, z_up)
+            send(above, w_dn + i, z_dn)
         else:
-            arrive(wb.at[0, x, 0, zb], w_up + 6)
-            arrive(wb.at[0, x, 1, za], w_dn + 6)
-            arrive(part(1, x, zb), w_up + 7)
-            weight_x(7)
-
-    xl, xr, xf = (x + 3) % 4, (x + 1) % 4, (x + 2) % 4
-    low = z < 4
+            send(below.at[0], w_up + i, z_up)
+            send(above.at[1], w_dn + i, z_dn)
+        weight_x(2 * i - 1)
+        weight_x(2 * i)
 
     def weight_x2(n):
-        for p in range(2):
-            arrive(part(p, xl, z_of(n)), x_up_ch + 2 * n + p)
-            arrive(part(p, xr, z_of(n)), x_dn_ch + 2 * n + p)
-            send(part(p, xl, z_of(n)), x2_ch + 2 * n + p, x_up, z >= 4)
-            send(part(p, xr, z_of(n)), x2_ch + 2 * n + p, x_dn, low)
-
-    def weight_y(n):
-        xx = (x, xl, xr, xf)[n]
-        if n == 3:
-            for m in range(8):
-                for p in range(2):
-                    arrive(part(p, xf, z_of(m)), x2_ch + 2 * m + p)
-        send(wb.at[1, xx, y], wy_ch + n, y_flip)
+        from_l, from_r = wb.at[xl, z_of(n)], wb.at[xr, z_of(n)]
+        arrive(from_l, x_up_ch + n)
+        arrive(from_r, x_dn_ch + n)
+        if n % 2:
+            send(from_r, x2_ch + n, x_dn)
+        else:
+            send(from_l, x2_ch + n, x_up, z >= 4)
+            send(from_r, x2_ch + n, x_dn, z < 4)
+
+    def second_x():
+        send(w2.at[z, x], p_up, x_up)
+        send(w2.at[z, x], p_dn, x_dn)
+
+    def second_x2():
+        arrive(w2.at[z, xl], p_up)
+        arrive(w2.at[z, xr], p_dn)
+        send(w2.at[z, xl], p_x2, x_up)
+
+    def second_z(i):
+        below, above = w2.at[(z + 8 - i) % 8], w2.at[(z + i) % 8]
+        if i == 0:
+            arrive(w2.at[z, xf], p_x2)
+            send(below, pz_up, z_up)
+            send(below, pz_dn, z_dn)
+            weight_y(0)
+            return
+        if i == 4:
+            arrive(below.at[pl.ds(0, 2)], pz_up + 3)
+            arrive(below.at[pl.ds(2, 2)], pz_dn + 3)
+            weight_y(7)
+            return
+        arrive(below, pz_up + i - 1)
+        arrive(above, pz_dn + i - 1)
+        send(below if i < 3 else below.at[pl.ds(0, 2)], pz_up + i, z_up)
+        send(above if i < 3 else above.at[pl.ds(2, 2)], pz_dn + i, z_dn)
+        weight_y(2 * i - 1)
+        weight_y(2 * i)
 
     qt = channel(4)
 
     def query_out():
         for d in range(1, GROUPS):
             col = pl.multiple_of(((g + d) % GROUPS) * WIDTH, HD)
-            send(q_in.at[:, pl.ds(col, WIDTH)], q_ch + d, peer(d), dst=qb.at[0, pl.ds(row0, 32)])
+            start(q_in.at[:, pl.ds(col, WIDTH)], qb.at[0, pl.ds(row0, 32)], q_ch, peer(d))
 
     def query_time():
-        for d in range(1, GROUPS):
-            src_row = pl.multiple_of(((g + GROUPS - d) % GROUPS) * 32, 32)
-            arrive(qb.at[0, pl.ds(src_row, 32)], q_ch + d)
+        arrive(qb.at[0, pl.ds(0, 224)], q_ch)
         send(qb.at[0], qt, t_up, later, dst=qb.at[1])
         send(bb.at[0], qt + 1, t_up, later, dst=bb.at[1])
         send(qb.at[0], qt + 2, t_dn, earlier, dst=qb.at[2])
         send(bb.at[0], qt + 3, t_dn, earlier, dst=bb.at[2])
 
     def weight_pair():
-        send(wb.at[0, x, y, z], w_y, y_flip)
+        send(wb.at[x, z, y], w_y, y_flip)
 
     do(weight_pair)
+    do(second_x)
     do(own_block, 0)
     do(query_out)
-    arrive(wb.at[0, x, 1 - y, z], w_y)
+    arrive(wb.at[x, z, 1 - y], w_y)
     do(weight_z, 0)
+    do(second_x2)
     do(own_block, 1)
     do(weight_z, 1)
     do(ring, 1, 0)
@@ -235,21 +253,22 @@
     do(ring, 2, 0)
     do(weight_z, 3)
     do(own_block, 2)
+    do(second_z, 0)
     do(weight_x2, 1)
     do(weight_x2, 2)
     do(ring, 1, 1)
     do(ring, 3, 0)
     do(weight_z, 4)
-    do(weight_y, 0)
     do(ring, 1, 2)
     do(weight_x2, 3)
-    do(weight_x2, 4)
     do(ring, 2, 1)
     do(ring, 4, 0)
+    do(weight_x2, 4)
+    do(second_z, 1)
+    do(ring, 3, 1)
+    do(ring, 2, 2)
     do(weight_x2, 5)
     do(weight_x2, 6)
-    do(ring, 3, 1)
-    do(ring, 2, 2)
 
     h_at = [h - (h + 3) // 4, h, h + 1 - h // 3]
     w_at = [w - (w + 3) // 4, w, w + 1 - w // 3]
@@ -276,7 +295,7 @@
         return m, acc
 
     po_ch, ps_ch = channel(6), channel(6)
-    a_ch, c_ch = channel(9), channel(12)
+    a_up, a_dn, far_up, far_dn, c_ch = channel(3), channel(3), channel(3), channel(3), channel()
     edge = ((1, earlier, t_dn), (2, later, t_up))
 
     def missing(k, cond):
@@ -293,7 +312,7 @@
                 copy(ps.at[k, a], rs.at[1 - k, a], ps_ch + 3 * k + a, dev))
 
     def feature(gg, a):
-        return ab.at[:, pl.ds(pl.multiple_of(gg * WIDTH + a * HD, HD), HD)]
+        return ab.at[HEADS_DEV * gg + a]
 
     def remote_unit(j, a):
         i, cond, dev = edge[j]
@@ -337,15 +356,29 @@
             num = num + ro[k, a].astype(jnp.float32) * f
             den = den + jnp.maximum(lk, 0.0) * f
         feature(g, a)[...] = (num / den).astype(jnp.bfloat16)
-        for d in range(1, 4):
-            share(g, a, a_ch + 3 * (d - 1) + a, peer(2 * d)).start()
-        share(g, a, c_ch + a, partner).start()
-
-    def relay(a):
-        for d in range(1, 4):
-            src = (g + GROUPS - 2 * d) % GROUPS
-            copy(feature(src, a), feature(src, a), a_ch + 3 * (d - 1) + a, z_up).wait_recv()
-            share(src, a, c_ch + 3 * d + a, partner).start()
+        for c in near(g, g, a):
+            c.start()
+        share(g, a, c_ch, partner).start()
+
+    def near(lower, upper, a):
+        return share(lower, a, a_up + a, peer(2)), share(upper, a, a_dn + a, peer(6))
+
+    def halves(lower, upper, a):
+        top, bottom = feature(lower, a).at[pl.ds(0, HD)], feature(upper, a).at[pl.ds(HD, HD)]
+        return copy(top, top, far_up + a, peer(2)), copy(bottom, bottom, far_dn + a, peer(6))
+
+    lower, upper, farther = (g + 6) % GROUPS, (g + 2) % GROUPS, (g + 4) % GROUPS
+
+    def relay_near(a):
+        for gg, came, on in zip((lower, upper), near(lower, upper, a), halves(lower, upper, a)):
+            came.wait_recv()
+            on.start()
+            share(gg, a, c_ch, partner).start()
+
+    def relay_far(a):
+        for came in halves(farther, farther, a):
+            came.wait_recv()
+        share(farther, a, c_ch, partner).start()
 
     arrive(qb.at[1], qt, earlier)
     arrive(bb.at[1], qt + 1, earlier)
@@ -367,7 +400,12 @@
 
         @pl.when(a == 0)
         def _():
+            do(second_z, 2)
             do(ring, 4, 1)
+
+        @pl.when(a == 1)
+        def _():
+            do(ring, 4, 2)
 
         remote_unit(1, a)
 
@@ -375,50 +413,52 @@
         def _():
             do(ring, 3, 2)
             do(weight_x2, 7)
+            do(second_z, 3)
 
         @pl.when(a > 0)
         def _():
             finish(a - 1)
 
+        @pl.when(a == 1)
+        def _():
+            do(second_z, 4)
+
+        @pl.when(a == 2)
+        def _():
+            relay_near(0)
+
         own_unit(a)
 
-        @pl.when(a == 0)
-        def _():
-            do(ring, 4, 2)
-            do(weight_y, 1)
-            do(weight_y, 2)
-
-        @pl.when(a == 1)
-        def _():
-            do(weight_y, 3)
-
-        @pl.when(a == 2)
-        def _():
-            relay(0)
-
         return 0
 
     lax.fori_loop(0, HEADS_DEV, head_step, 0)
+    relay_near(1)
     finish(HEADS_DEV - 1)
-    relay(1)
-    for n, xx in enumerate((x, xl, xr, xf)):
-        arrive(wb.at[1, xx, 1 - y], wy_ch + n)
-    relay(2)
-    for a in range(HEADS_DEV):
-        for d in range(4):
-            src = (g + 1 - 2 * core + GROUPS - 2 * d) % GROUPS
-            copy(feature(src, a), feature(src, a), c_ch + 3 * d + a, z_up).wait_recv()
-
-    for n in range(3):
-        acc = jnp.zeros((TILE, 256), jnp.float32)
-        for j in range(GROUPS):
-            if n == 1:
-                rows = jnp.concatenate([wb[0, j % 4, j // 4, :, :, 256:], wb[1, j % 4, j // 4, :, :, :128]], axis=2)
-            else:
-                rows = wb[n // 2, j % 4, j // 4, :, :, (0, 0, 128)[n] : (256, 0, 384)[n]]
-            acc = acc + jnp.dot(ab[:, j * WIDTH : (j + 1) * WIDTH], rows.reshape(WIDTH, 256),
-                                preferred_element_type=jnp.float32)
-        out_ref[:, n * 256 : n * 256 + 256] = acc.astype(jnp.bfloat16)
+    relay_far(0)
+    relay_far(1)
+    for n in range(8):
+        arrive(wb.at[xf, z_of(n)], x2_ch + n)
+    arrive(wf, wy_ch)
+    relay_near(2)
+    relay_far(2)
+    twelve = ab.at[pl.ds(0, 12)]
+    copy(twelve, twelve, c_ch, z_up).wait_recv()
+
+    def wide(gg):
+        return jnp.concatenate([ab[HEADS_DEV * gg + a] for a in range(HEADS_DEV)], axis=1)
+
+    for half in range(2):
+        acc = jnp.zeros((TILE, WIDTH), jnp.float32)
+        for j in range(4):
+            for k in range(2):
+                if half == 0:
+                    left, rows = wide(4 * k + j), wb[j, :, k]
+                elif k == 0:
+                    left, rows = wide(4 * y + j), w2[:, j]
+                else:
+                    left, rows = wide(4 - 4 * y + j), wf[:, j]
+                acc = acc + jnp.dot(left, rows.reshape(WIDTH, WIDTH), preferred_element_type=jnp.float32)
+        out_ref[:, half * WIDTH : (half + 1) * WIDTH] = acc.astype(jnp.bfloat16)
 
     draining[0] = True
     for step, which in done:
@@ -427,11 +467,13 @@
         for i, cond, dev in edge:
             for c in back(i - 1, a, dev):
                 pl.when(cond)(c.wait_send)
-        for d in range(1, 4):
-            share(g, a, a_ch + 3 * (d - 1) + a, peer(2 * d)).wait_send()
-        for d in range(4):
-            share(g, a, c_ch + 3 * d + a, partner).wait_send()
-    assert channels[0] <= N_CH
+        for c in near(g, g, a) + halves(lower, upper, a):
+            c.wait_send()
+    copy(twelve, twelve, c_ch, partner).wait_send()
+    copy(wf, wf, wy_ch, y_flip).wait_send()
+    sevenths = qb.at[0, pl.ds(0, 224)]
+    copy(sevenths, sevenths, q_ch, partner).wait_send()
+    assert channels[0] == N_CH, channels[0]
 
 
 def local(queries, keys, values, window, out_weight):
@@ -444,10 +486,12 @@
         out_specs=pl.BlockSpec(memory_space=pltpu.VMEM),
         scratch_shapes=[
             pltpu.VMEM((16, HEADS_DEV, 2, TILE, HD), bf16),
-            pltpu.VMEM((2, 4, 2, 8, 48, WIDTH), bf16),
+            pltpu.VMEM((4, 8, 2, 48, WIDTH), bf16),
+            pltpu.VMEM((8, 4, 48, WIDTH), bf16),
+            pltpu.VMEM((8, 4, 48, WIDTH), bf16),
             pltpu.VMEM((3, TILE, WIDTH), bf16),
             pltpu.VMEM((3, 32, HD), f32),
-            pltpu.VMEM((TILE, GROUPS * WIDTH), bf16),
+            pltpu.VMEM((GROUPS * HEADS_DEV, TILE, HD), bf16),
             pltpu.VMEM((9, TILE, TILE), f32),
             pltpu.VMEM((2, HEADS_DEV, TILE, HD), bf16),
             pltpu.VMEM((2, HEADS_DEV, 8, TILE), f32),

time: 111 us -> 101 us (0.910)
  Pallas kernels: 109 us -> 98.8 us
    pallas_call x1, Pallas kernels: 109 us -> 98.8 us  [local(): pl.pallas_call(kernel, out_shape=jax.ShapeDtypeStruct((TILE, out_weight.s...]
where the time goes in v4:
time: 101 us
  Pallas kernels  98.8 us (98%)
  local copies, waits for them, and re-layouts  1.77 us (2%)
    pallas_call x1, Pallas kernels, local(): pl.pallas_call(kernel, out_shape=jax.ShapeDtypeStruct((TILE, out_weight.s...  98.8 us

profile of v4, /device:TPU:5, one launch (start us, length us, event | category | flops | bytes accessed | tf_op | source)
XLA Modules:
  0.0 100.6 jit_solution(13435935043113400561)
XLA Ops:
  0.0 98.8 %shard_map.55 = bf16[256,768]{1,0:T(8,128)(2,1)} custom-call(bf16[32,3072]{1,0:T(8,128)(2,1)} %q_in.1, bf16[256,384]{1,0:T(8,128)(2,1)} %k_in.1, bf16[256,384]{1,0:T(8,128)(2,1)} %v_in.1, s32[1,27]{1,0:T(1,128)} %win.1, bf16[48,768]{1,0:T(8,128)(2,1)} %w_in.1), custom_call_target="tpu_custom_call" | custom-call | tf_op jit(solution)/shard_map/pallas_call | solution.py:482
  98.8 1.8 %copy.7 = bf16[256,768]{1,0:T(8,128)(2,1)} copy(bf16[256,768]{1,0:T(8,128)(2,1)} %shard_map.55) | data formatting | bytes 786432

commit v5 on v4

--- a/solution.py
+++ b/solution.py
@@ -16,11 +16,11 @@
 NEG = -1e30
 BIG = 1e30
 SCALE = 1.4426950408889634 * HD**-0.5
-N_CH = 108
+N_CH = 109
 
 
 def kernel(q_in, k_in, v_in, win, w_in, out_ref,
-           kv, wb, w2, wf, qb, bb, ab, sb, po, ps, ro, rs, lo, ls, send_sem, recv_sem, loc_sem):
+           kv, wb, w2, wf, qb, bb, ab, sb, po, ps, ro, rs, lo, ls, part_sum, send_sem, recv_sem, loc_sem):
     s = lax.axis_index("seq")
     g = lax.axis_index("head")
     y = s // 32
@@ -100,10 +100,6 @@
     local.append(pltpu.make_async_copy(q_in.at[:, pl.ds(col0, WIDTH)], qb.at[0, pl.ds(row0, 32)], loc_sem.at[8]))
     for c in local:
         c.start()
-    for n in range(27):
-        bb[0, n : n + 1, :] = jnp.full((1, HD), jnp.where(win[0, n] >= 0, 0.0, BIG), jnp.float32)
-    for c in local:
-        c.wait()
     pl.semaphore_wait(barrier, len(greeted))
 
     up, dn = channel(12) - 3, channel(12) - 3
@@ -237,10 +233,18 @@
     def weight_pair():
         send(wb.at[x, z, y], w_y, y_flip)
 
+    for c in local[:2]:
+        c.wait()
+    do(own_block, 0)
+    for c in local[6:8]:
+        c.wait()
     do(weight_pair)
     do(second_x)
-    do(own_block, 0)
     do(query_out)
+    for n in range(27):
+        bb[0, n : n + 1, :] = jnp.full((1, HD), jnp.where(win[0, n] >= 0, 0.0, BIG), jnp.float32)
+    for c in local[2:6] + local[8:]:
+        c.wait()
     arrive(wb.at[x, z, 1 - y], w_y)
     do(weight_z, 0)
     do(second_x2)
@@ -295,7 +299,7 @@
         return m, acc
 
     po_ch, ps_ch = channel(6), channel(6)
-    a_up, a_dn, far_up, far_dn, c_ch = channel(3), channel(3), channel(3), channel(3), channel()
+    a_up, a_dn, far_up, far_dn, c_ch = channel(3), channel(3), channel(3), channel(3), channel(2)
     edge = ((1, earlier, t_dn), (2, later, t_up))
 
     def missing(k, cond):
@@ -358,7 +362,7 @@
         feature(g, a)[...] = (num / den).astype(jnp.bfloat16)
         for c in near(g, g, a):
             c.start()
-        share(g, a, c_ch, partner).start()
+        share(g, a, c_ch + a // 2, partner).start()
 
     def near(lower, upper, a):
         return share(lower, a, a_up + a, peer(2)), share(upper, a, a_dn + a, peer(6))
@@ -373,12 +377,12 @@
         for gg, came, on in zip((lower, upper), near(lower, upper, a), halves(lower, upper, a)):
             came.wait_recv()
             on.start()
-            share(gg, a, c_ch, partner).start()
+            share(gg, a, c_ch + a // 2, partner).start()
 
     def relay_far(a):
         for came in halves(farther, farther, a):
             came.wait_recv()
-        share(farther, a, c_ch, partner).start()
+        share(farther, a, c_ch + a // 2, partner).start()
 
     arrive(qb.at[1], qt, earlier)
     arrive(bb.at[1], qt + 1, earlier)
@@ -440,25 +444,33 @@
         arrive(wb.at[xf, z_of(n)], x2_ch + n)
     arrive(wf, wy_ch)
     relay_near(2)
-    relay_far(2)
-    twelve = ab.at[pl.ds(0, 12)]
-    copy(twelve, twelve, c_ch, z_up).wait_recv()
-
-    def wide(gg):
-        return jnp.concatenate([ab[HEADS_DEV * gg + a] for a in range(HEADS_DEV)], axis=1)
-
-    for half in range(2):
+    eight, four = ab.at[pl.ds(0, 8)], ab.at[pl.ds(0, 4)]
+    copy(eight, eight, c_ch, z_up).wait_recv()
+
+    def wide(gg, heads):
+        return jnp.concatenate([ab[HEADS_DEV * gg + a] for a in heads], axis=1)
+
+    def project(half, heads):
+        rows_at = slice(heads[0] * HD, (heads[-1] + 1) * HD)
         acc = jnp.zeros((TILE, WIDTH), jnp.float32)
         for j in range(4):
             for k in range(2):
                 if half == 0:
-                    left, rows = wide(4 * k + j), wb[j, :, k]
+                    left, rows = wide(4 * k + j, heads), wb[j, :, k]
                 elif k == 0:
-                    left, rows = wide(4 * y + j), w2[:, j]
+                    left, rows = wide(4 * y + j, heads), w2[:, j]
                 else:
-                    left, rows = wide(4 - 4 * y + j), wf[:, j]
-                acc = acc + jnp.dot(left, rows.reshape(WIDTH, WIDTH), preferred_element_type=jnp.float32)
-        out_ref[:, half * WIDTH : (half + 1) * WIDTH] = acc.astype(jnp.bfloat16)
+                    left, rows = wide(4 - 4 * y + j, heads), wf[:, j]
+                acc = acc + jnp.dot(left, rows.reshape(WIDTH, WIDTH)[rows_at], preferred_element_type=jnp.float32)
+        return acc
+
+    for half in range(2):
+        part_sum[half] = project(half, (0, 1))
+    relay_far(2)
+    copy(four, four, c_ch + 1, z_up).wait_recv()
+    for half in range(2):
+        total = part_sum[half] + project(half, (2,))
+        out_ref[:, half * WIDTH : (half + 1) * WIDTH] = total.astype(jnp.bfloat16)
 
     draining[0] = True
     for step, which in done:
@@ -469,7 +481,8 @@
                 pl.when(cond)(c.wait_send)
         for c in near(g, g, a) + halves(lower, upper, a):
             c.wait_send()
-    copy(twelve, twelve, c_ch, partner).wait_send()
+    copy(eight, eight, c_ch, partner).wait_send()
+    copy(four, four, c_ch + 1, partner).wait_send()
     copy(wf, wf, wy_ch, y_flip).wait_send()
     sevenths = qb.at[0, pl.ds(0, 224)]
     copy(sevenths, sevenths, q_ch, partner).wait_send()
@@ -499,6 +512,7 @@
             pltpu.VMEM((2, HEADS_DEV, 8, TILE), f32),
             pltpu.VMEM((2, TILE, 2 * HD), f32),
             pltpu.VMEM((2, TILE, HD), f32),
+            pltpu.VMEM((2, TILE, WIDTH), f32),
             pltpu.SemaphoreType.DMA((N_CH,)),
             pltpu.SemaphoreType.DMA((N_CH,)),
             pltpu.SemaphoreType.DMA((9,)),

time: 101 us -> 99.9 us (0.989)
  no operation moved by 1% of the time
where the time goes in v5:
time: 99.9 us; the launch traced here: 99.8 us
  Pallas kernels  98 us (98%)
  local copies, waits for them, and re-layouts  1.77 us (2%)
    pallas_call x1, Pallas kernels, local(): pl.pallas_call(kernel, out_shape=jax.ShapeDtypeStruct((TILE, out_weight.s...  98 us

profile of v5, /device:TPU:5, one launch (start us, length us, event | category | flops | bytes accessed | tf_op | source)
XLA Modules:
  0.0 99.8 jit_solution(2691238970717100498)
XLA Ops:
  0.0 98.0 %shard_map.55 = bf16[256,768]{1,0:T(8,128)(2,1)} custom-call(bf16[32,3072]{1,0:T(8,128)(2,1)} %q_in.1, bf16[256,384]{1,0:T(8,128)(2,1)} %k_in.1, bf16[256,384]{1,0:T(8,128)(2,1)} %v_in.1, s32[1,27]{1,0:T(1,128)} %win.1, bf16[48,768]{1,0:T(8,128)(2,1)} %w_in.1), custom_call_target="tpu_custom_call" | custom-call | tf_op jit(solution)/shard_map/pallas_call | solution.py:495
  98.0 1.8 %copy.7 = bf16[256,768]{1,0:T(8,128)(2,1)} copy(bf16[256,768]{1,0:T(8,128)(2,1)} %shard_map.55) | data formatting | bytes 786432
